TPU v7x, 256 devices: a whole 4x4x8 slice. The times are simulated.
256 devices in a mesh: narrow: 8 (over x, core), wide: 32 (over y, z).
Axes of the slice: x: 4, y: 4, z: 8, core: 2. Of those that a mesh axis runs over, the one named last changes fastest.
Arguments:
- start_block: bfloat16 [8, 32, 32, 3584], P('narrow', 'wide'), may hold values from -360 to 360
- weights: bfloat16 [8, 32, 28, 12, 128, 128], P('narrow', 'wide'), may hold values from 0.049804688 to 1
- pattern: int32 [8, 32, 28, 12], P('narrow', 'wide'), may hold values from 0 to 33, as said below
Outputs:
- filtered_basis: float32 [8, 32, 32, 3584], P('narrow', 'wide')
Inputs may be any that keep to these rules, and one draw needn't show every extreme that they name: `pattern`: slot 0 of each row block names the block itself; slots below 9, and every slot of blocks from 24 on, name blocks of the own tile; the other slots of a rim block name block value - 28 of the facing neighbour's rim that faces it.
All inputs are finite; a program needn't handle non-finite values.
Results may differ from a plain program's by a relative error of at most 0.0031.
Values may be sent and summed in bfloat16 or wider, within the bound.
A program may use at most 64 MiB of HBM per device.

v0:
```python
import math

import jax
import jax.numpy as jnp
import numpy as np
from jax import lax
from jax.experimental import pallas as pl
from jax.experimental.pallas import tpu as pltpu
from jax.sharding import PartitionSpec as P

f32 = jnp.float32
bf16 = jnp.bfloat16
i32 = jnp.int32
MESH = pl.DeviceIdType.MESH

NVEC = 32
BS = 128
K = 12
K_IN = 9
RIM = 6
BLK = 28
RIM_ROWS = 4 * RIM
LOWER = 0.3
CENTER = (2.0 + LOWER) / 2.0
HALF = (2.0 - LOWER) / 2.0
OPP = (1, 0, 3, 2)

N_OWN = RIM_ROWS * K_IN + (BLK - RIM_ROWS) * K
N_RIM = RIM_ROWS * (K - K_IN)
OWN_PAIRS = (N_OWN + BLK) // 2
RIM_PAIRS = (N_RIM // 4 + RIM) // 2
T_GROUPS = 2
Z_CHIPS = 8
Y_CHIPS = 4

O_OW = 0
O_OU = O_OW + 2 * OWN_PAIRS
O_RW = O_OU + 2 * OWN_PAIRS
O_RU = O_RW + 8 * RIM_PAIRS
O_OE = O_RU + 8 * RIM_PAIRS
O_RE = O_OE + BLK
O_PT = O_RE + RIM_ROWS
F_OF = 0
F_RF = F_OF + OWN_PAIRS
F_NE = F_RF + 4 * RIM_PAIRS


def own_index(b):
    return b * K_IN if b < RIM_ROWS else RIM_ROWS * K_IN + (b - RIM_ROWS) * K


def sorted_lists(target, segments, group, base, pairs_total):
    count = target.shape[0]
    seg = np.arange(segments)
    hot = (target[:, None] == jnp.asarray(seg, i32)[None, :]).astype(i32)
    cnt = hot.sum(0)
    pairs = (cnt + 1) // 2
    before = jnp.asarray((seg[:, None] < seg[None, :]) & (seg[:, None] // group == seg[None, :] // group), i32)
    start = jnp.asarray(base, i32) + (pairs[:, None] * before).sum(0)
    order = np.arange(count)
    earlier = jnp.asarray(order[None, :] < order[:, None])
    rank = ((target[:, None] == target[None, :]) & earlier).astype(i32).sum(1)
    pos = (hot * (2 * start)[None, :]).sum(1) + rank
    place = jnp.arange(2 * pairs_total, dtype=i32)
    entry = jnp.where(place[:, None] == pos[None, :], jnp.asarray(order + 1, i32)[None, :], 0).sum(1)
    pair_ids = jnp.arange(pairs_total, dtype=i32)
    keep = 1 - (pair_ids[:, None] == start[None, :]).any(1).astype(i32)
    end = jnp.maximum(start + pairs - 1, 0)
    return entry, keep, end, cnt


def tables(pattern):
    own_target = jnp.concatenate([pattern[:RIM_ROWS, :K_IN].reshape(-1), pattern[RIM_ROWS:].reshape(-1)])
    rim_rows = np.repeat(np.arange(RIM_ROWS), K - K_IN)
    rim_target = pattern[:RIM_ROWS, K_IN:].reshape(-1) - BLK + jnp.asarray(rim_rows // RIM * RIM, i32)
    entry, keep, end, _ = sorted_lists(own_target, BLK, BLK, np.zeros(BLK), OWN_PAIRS)
    ow = jnp.maximum(entry - 1, 0)
    ob = jnp.where(ow < RIM_ROWS * K_IN, ow // K_IN, RIM_ROWS + (ow - RIM_ROWS * K_IN) // K)
    ou = jnp.where(entry > 0, ob, BLK)
    rbase = np.arange(RIM_ROWS) // RIM * RIM_PAIRS
    rentry, rkeep, rend, rcnt = sorted_lists(rim_target, RIM_ROWS, RIM, rbase, 4 * RIM_PAIRS)
    rw = jnp.maximum(rentry - 1, 0)
    ru = jnp.where(rentry > 0, rw // (K - K_IN), BLK)
    facing = jnp.asarray(np.arange(BLK) // RIM * RIM - BLK, i32)[:, None]
    source = jnp.where(pattern < BLK, pattern, pattern + facing)
    ints = jnp.concatenate([ow, ou, rw, ru, end, rend, source.reshape(-1)]).astype(i32)
    floats = jnp.concatenate([keep, rkeep, (rcnt > 0).astype(i32)]).astype(f32)
    return ints, floats


def kernel(
    tab, ftab, start_ref, w_hbm, out_ref,
    wo, wr, wto, wtr, u, ones, rim, recv_v, recv_t, send_t, recv_d, send_d,
    cur, prev, acc, inv, run_o, run_r, pack, ar1, ar2, ar3,
    w_sem, vs, vr, ts, tr, ds, dr, s1, r1, s2, r2, s3, r3,
):
    ni = lax.axis_index("narrow")
    wi = lax.axis_index("wide")
    n_narrow = lax.axis_size("narrow")
    n_wide = lax.axis_size("wide")
    north = lax.rem(ni + n_narrow - 1, n_narrow)
    south = lax.rem(ni + 1, n_narrow)
    west = lax.rem(wi + n_wide - 1, n_wide)
    east = lax.rem(wi + 1, n_wide)
    neighbours = ({"narrow": north}, {"narrow": south}, {"wide": west}, {"wide": east})
    has = (ni > 0, ni < n_narrow - 1, wi > 0, wi < n_wide - 1)
    wy = wi // Z_CHIPS
    wz = lax.rem(wi, Z_CHIPS)
    group1 = [{"narrow": lax.rem(ni + k, n_narrow)} for k in range(1, 8)]
    group2 = [{"wide": lax.rem(wi + k * Z_CHIPS, n_wide)} for k in range(1, Y_CHIPS)]
    group3 = [{"wide": wy * Z_CHIPS + lax.rem(wz + k, Z_CHIPS)} for k in range(1, Z_CHIPS)]

    barrier = pltpu.get_barrier_semaphore()
    greeted = [{"wide": west}, {"wide": east}] + group1 + group2 + group3
    for peer in greeted:
        pl.semaphore_signal(barrier, inc=1, device_id=peer, device_id_type=MESH)

    rim_copies = []
    for b in range(RIM_ROWS):
        n = K - K_IN
        rim_copies.append(pltpu.make_async_copy(
            w_hbm.at[pl.ds(b * K + K_IN, n)], wr.at[pl.ds(b * n, n)], w_sem.at[b]))
    own_copies = []
    for b in range(BLK):
        n = K_IN if b < RIM_ROWS else K
        own_copies.append(pltpu.make_async_copy(
            w_hbm.at[pl.ds(b * K, n)], wo.at[pl.ds(own_index(b), n)], w_sem.at[RIM_ROWS + b]))
    for copy in rim_copies + own_copies:
        copy.start()

    ones[...] = jnp.ones_like(ones)
    ones[BLK] = jnp.zeros_like(ones[BLK])
    for a in range(3):
        u[a, BLK] = jnp.zeros((NVEC, BS), bf16)

    def pair_product(lhs, w, ow, ou, q):
        left = jnp.concatenate([lhs(tab[ou + 2 * q]), lhs(tab[ou + 2 * q + 1])], axis=1)
        right = jnp.concatenate([w[tab[ow + 2 * q]], w[tab[ow + 2 * q + 1]]], axis=0)
        return jnp.dot(left, right, preferred_element_type=f32)

    def rim_out(lhs, rows, put):
        for d in range(4):
            run = None
            for q in range(d * RIM_PAIRS, (d + 1) * RIM_PAIRS):
                part = pair_product(lhs, wr, O_RW, O_RU, q)
                run = part if run is None else run * ftab[F_RF + q] + part
                run_r[q, 0:rows] = run
            for j in range(RIM):
                e = d * RIM + j
                put(d, j, (run_r[tab[O_RE + e], 0:rows] * ftab[F_NE + e]).astype(bf16))

    def own_back(lhs, rows):
        per = OWN_PAIRS // T_GROUPS

        def body(g, run):
            for q in range(per):
                at = g * per + q
                part = pair_product(lhs, wo, O_OW, O_OU, at)
                run = run * ftab[F_OF + at] + part
                run_o[at, 0:rows] = run
            return run

        lax.fori_loop(0, T_GROUPS, body, jnp.zeros((rows, BS), f32))

    for copy in rim_copies:
        copy.wait()
    for k in range(N_RIM):
        wtr[k] = wr[k].T

    def put_degree(d, j, value):
        send_d[d, j] = value[0:8]

    rim_out(lambda k: ones[k], 16, put_degree)
    pl.semaphore_wait(barrier, len(greeted))
    degree_copies = []
    for d in (2, 3, 0, 1):
        copy = pltpu.make_async_remote_copy(
            send_d.at[d], recv_d.at[OPP[d]], ds.at[d], dr.at[OPP[d]],
            device_id=neighbours[d], device_id_type=MESH)
        copy.start()
        degree_copies.append(copy)

    ones_wide = jnp.ones((16, K * BS), bf16)
    for b in range(BLK):
        n = K_IN if b < RIM_ROWS else K
        o = own_index(b)
        own_copies[b].wait()
        for s in range(n):
            wto[o + s] = wo[o + s].T
        total = jnp.dot(ones_wide[:, : n * BS], wto[o : o + n].reshape(n * BS, BS), preferred_element_type=f32)
        if b < RIM_ROWS:
            m = K - K_IN
            side = jnp.dot(ones_wide[:, : m * BS], wtr[b * m : b * m + m].reshape(m * BS, BS), preferred_element_type=f32)
            total = total + jnp.where(has[b // RIM], side, 0.0)
        inv[b] = total[0:8]
    own_back(lambda k: ones[k], 16)
    for copy in degree_copies:
        copy.wait_recv()
    for b in range(BLK):
        deg = inv[b] + run_o[tab[O_OE + b], 0:8]
        if b < RIM_ROWS:
            deg = deg + jnp.where(has[b // RIM], recv_d[b // RIM, b % RIM].astype(f32), 0.0)
        inv[b] = 1.0 / jnp.sqrt(0.5 * deg)
        x = start_ref[:, b * BS : (b + 1) * BS].astype(f32)
        cur[b] = x
        prev[b] = x
        u[0, b] = (inv[b, 0:1] * x).astype(bf16)
    for copy in degree_copies:
        copy.wait_send()

    def step(a, carry):
        copies = []
        for d in (2, 3, 0, 1):
            copy = pltpu.make_async_remote_copy(
                u.at[a, pl.ds(d * RIM, RIM)], recv_v.at[a, OPP[d]], vs.at[a, d], vr.at[a, OPP[d]],
                device_id=neighbours[d], device_id_type=MESH)
            copy.start()
            copies.append(copy)

        def put_terms(d, j, value):
            send_t[a, d, j] = value

        rim_out(lambda k: u[a, k], NVEC, put_terms)
        term_copies = []
        for d in (2, 3, 0, 1):
            copy = pltpu.make_async_remote_copy(
                send_t.at[a, d], recv_t.at[a, OPP[d]], ts.at[a, d], tr.at[a, OPP[d]],
                device_id=neighbours[d], device_id_type=MESH)
            copy.start()
            term_copies.append(copy)
        own_back(lambda k: u[a, k], NVEC)
        for b in range(BLK):
            n = K_IN if b < RIM_ROWS else K
            o = own_index(b)
            left = jnp.concatenate([u[a, tab[O_PT + b * K + s]] for s in range(n)], axis=1)
            ahead = jnp.dot(left, wto[o : o + n].reshape(n * BS, BS), preferred_element_type=f32)
            acc[b] = ahead + run_o[tab[O_OE + b]]
        for copy in copies:
            copy.wait_recv()
        for d in range(4):
            for j in range(RIM):
                rim[d * RIM + j] = jnp.where(has[d], recv_v[a, d, j], jnp.zeros((NVEC, BS), bf16))
        for b in range(RIM_ROWS):
            m = K - K_IN
            d = b // RIM
            left = jnp.concatenate([rim[tab[O_PT + b * K + K_IN + s]] for s in range(m)], axis=1)
            acc[b] += jnp.dot(left, wtr[b * m : b * m + m].reshape(m * BS, BS), preferred_element_type=f32)
        for copy in term_copies:
            copy.wait_recv()
        alpha = jnp.where(a == 0, 1.0, 2.0).astype(f32) / HALF
        beta = jnp.where(a == 0, 0.0, 1.0).astype(f32)
        nxt = lax.rem(a + 1, 3)
        for b in range(BLK):
            total = acc[b]
            if b < RIM_ROWS:
                total = total + jnp.where(has[b // RIM], recv_t[a, b // RIM, b % RIM].astype(f32), 0.0)
            root = inv[b, 0:1]
            y = cur[b]
            new = alpha * ((y - (0.5 * root) * total) - CENTER * y) - beta * prev[b]
            prev[b] = y
            cur[b] = new
            acc[b] = root * new
        for copy in copies + term_copies:
            copy.wait_send()
        for b in range(BLK):
            u[nxt, b] = acc[b].astype(bf16)
        return carry

    lax.fori_loop(0, 3, step, 0)

    highs = [cur[b].astype(bf16) for b in range(BLK)]
    lows = [(cur[b] - highs[b].astype(f32)).astype(bf16) for b in range(BLK)]
    stacked = jnp.concatenate([jnp.concatenate(highs, axis=1), jnp.concatenate(lows, axis=1)], axis=0)
    product = lax.dot_general(stacked, stacked, (((1,), (1,)), ((), ())), preferred_element_type=f32)
    gram = product[:NVEC, :NVEC] + product[NVEC:, NVEC:] + product[:NVEC, NVEC:] + product[NVEC:, :NVEC]
    packed = jnp.concatenate([gram[8 * g : 8 * g + 8] for g in range(4)], axis=1)

    for group, landing, sends, recvs in ((group1, ar1, s1, r1), (group2, ar2, s2, r2), (group3, ar3, s3, r3)):
        slot = {id(ar1): 0, id(ar2): 1, id(ar3): 2}[id(landing)]
        pack[slot] = packed
        sent = []
        for k, peer in enumerate(group):
            copy = pltpu.make_async_remote_copy(
                pack.at[slot], landing.at[k], sends.at[k], recvs.at[k],
                device_id=peer, device_id_type=MESH)
            copy.start()
            sent.append(copy)
        for copy in sent:
            copy.wait_recv()
        for k in range(len(group)):
            packed = packed + landing[k]
        for copy in sent:
            copy.wait_send()

    lane = lax.broadcasted_iota(i32, (NVEC, BS), 1)
    row = lax.broadcasted_iota(i32, (NVEC, BS), 0)
    moved = jnp.concatenate([pltpu.roll(packed, (96 - 32 * g) % 128, 1) for g in range(4)], axis=0)
    m = jnp.where(lane >= 96, moved, jnp.where(lax.rem(lane, 32) == row, 1.0, 0.0))
    roots = jnp.zeros((NVEC, BS), f32)
    for k in range(NVEC):
        pivot = m[k : k + 1, :]
        d = jnp.broadcast_to(pivot[:, 96 + k : 97 + k], (1, BS))
        column = jnp.broadcast_to(m[:, 96 + k : 97 + k], (NVEC, BS))
        roots = jnp.where(row == k, lax.rsqrt(d), roots)
        m = m - jnp.where(row > k, column, 0.0) * (pivot * (1.0 / d))
    count = n_narrow * n_wide * BLK * BS
    solve = m * roots * math.sqrt(count)
    solve_high = solve.astype(bf16)
    solve_low = (solve - solve_high.astype(f32)).astype(bf16)
    left = jnp.where((lane >= 32) & (lane < 64), solve_low.astype(f32), solve_high.astype(f32))
    left = jnp.where(lane < 96, left, 0.0).astype(bf16)
    for b in range(BLK):
        right = jnp.concatenate([highs[b], highs[b], lows[b], lows[b]], axis=0)
        out_ref[:, b * BS : (b + 1) * BS] = jnp.dot(left, right, preferred_element_type=f32)


def body(start_block, weights, pattern):
    ints, floats = tables(pattern[0, 0])
    dma = pltpu.SemaphoreType.DMA
    vmem = pltpu.VMEM
    out = pl.pallas_call(
        kernel,
        out_shape=jax.ShapeDtypeStruct((NVEC, BLK * BS), f32),
        in_specs=[
            pl.BlockSpec(memory_space=pltpu.SMEM),
            pl.BlockSpec(memory_space=pltpu.SMEM),
            pl.BlockSpec(memory_space=pltpu.VMEM),
            pl.BlockSpec(memory_space=pl.ANY),
        ],
        out_specs=pl.BlockSpec(memory_space=pltpu.VMEM),
        scratch_shapes=[
            vmem((N_OWN, BS, BS), bf16),
            vmem((N_RIM, BS, BS), bf16),
            vmem((N_OWN, BS, BS), bf16),
            vmem((N_RIM, BS, BS), bf16),
            vmem((3, BLK + 1, NVEC, BS), bf16),
            vmem((BLK + 1, 16, BS), bf16),
            vmem((RIM_ROWS, NVEC, BS), bf16),
            vmem((3, 4, RIM, NVEC, BS), bf16),
            vmem((3, 4, RIM, NVEC, BS), bf16),
            vmem((3, 4, RIM, NVEC, BS), bf16),
            vmem((4, RIM, 8, BS), bf16),
            vmem((4, RIM, 8, BS), bf16),
            vmem((BLK, NVEC, BS), f32),
            vmem((BLK, NVEC, BS), f32),
            vmem((BLK, NVEC, BS), f32),
            vmem((BLK, 8, BS), f32),
            vmem((OWN_PAIRS, NVEC, BS), f32),
            vmem((4 * RIM_PAIRS, NVEC, BS), f32),
            vmem((3, 8, BS), f32),
            vmem((7, 8, BS), f32),
            vmem((3, 8, BS), f32),
            vmem((7, 8, BS), f32),
            dma((RIM_ROWS + BLK,)),
            dma((3, 4)),
            dma((3, 4)),
            dma((3, 4)),
            dma((3, 4)),
            dma((4,)),
            dma((4,)),
            dma((7,)),
            dma((7,)),
            dma((3,)),
            dma((3,)),
            dma((7,)),
            dma((7,)),
        ],
        compiler_params=pltpu.CompilerParams(
            collective_id=0, has_side_effects=True, vmem_limit_bytes=56 * 2**20
        ),
        name="filter_step",
    )(ints, floats, start_block[0, 0], weights.reshape(BLK * K, BS, BS))
    return out.reshape(1, 1, NVEC, BLK * BS)


def solution(mesh):
    placed = (
        P("narrow", "wide", None, None),
        P("narrow", "wide", None, None, None, None),
        P("narrow", "wide", None, None),
    )
    return jax.shard_map(
        body, mesh=mesh, in_specs=placed, out_specs=P("narrow", "wide", None, None), check_vma=False
    )
```

profile of v0, /device:TPU:1, one launch (start us, length us, event | category | flops | bytes accessed | tf_op | source)
XLA Modules:
  0.0 67.0 jit_solution(11168286875643871365)
XLA Ops:
  0.0 0.8 %slice.11 = s32[1,1,4,12]{2,1,3,0:T(1,128)S(1)} slice(s32[1,1,28,12]{2,1,3,0:T(1,128)} %param.17), slice={[0:1], [0:1], [24:28], [0:12]} | slice | bytes 384 | tf_op jit(solution)/shard_map/slice | solution.py:73
  0.8 0.1 copy.23
  0.9 0.1 reshape.80
  0.9 0.7 %copy.28 = s32[1,1,28,12]{2,3,1,0:T(8,128)S(1)} copy(s32[1,1,28,12]{2,1,3,0:T(1,128)} %param.17) | data formatting | bytes 2688
  1.6 0.7 %fusion.11 = s32[24,3]{0,1:T(4,128)S(1)} fusion(s32[24,3]{0,1:T(4,128)} %constant.116, s32[28,12]{0,1:T(8,128)S(1)} %bitcast.10), kind=kLoop, calls=%fused_computation.28 | loop fusion | flops 144 | bytes 864 | tf_op jit(solution)/shard_map/add | solution.py:75
  2.3 0.1 copy.24
  2.4 0.1 reshape.84
  2.5 0.1 fusion.7
  2.7 0.8 %multiply_reduce_fusion.1 = s32[24]{0:T(128)S(1)} fusion(s32[24,24]{1,0:T(8,128)} %constant.108.clone, s32[24]{0:T(128)S(1)} %and_select_fusion.1), kind=kLoop, calls=%fused_computation.20 | loop fusion | flops 1128 | bytes 2496 | tf_op jit(solution)/shard_map/reduce_sum | solution.py:59
  3.5 0.7 add_maximum_fusion.1
  4.1 0.1 fusion.9
  4.2 0.1 fusion.8
  4.3 0.9 %convert_reduce_fusion.1 = s32[72]{0:T(128)S(1)} fusion(pred[72,72]{1,0:T(8,128)(4,1)} %constant.110.clone, s32[72]{0:T(128)S(1)} %reshape.84), kind=kLoop, calls=%fused_computation.9 | loop fusion | flops 20664 | bytes 5760 | tf_op jit(solution)/shard_map/reduce_sum | solution.py:62
  5.2 0.8 %select_reduce_fusion.1 = s32[96]{0:T(128)S(1)} fusion(s32[72]{0:T(128)} %constant.111.clone, s32[72]{0:T(128)S(1)} %add.88), kind=kLoop, calls=%fused_computation.8 | loop fusion | flops 20640 | bytes 960 | tf_op jit(solution)/shard_map/reduce_sum | solution.py:65
  6.0 0.1 copy.22
  6.1 0.1 reshape.79
  6.2 0.1 pad_add_fusion
  6.3 0.1 fusion.2
  6.4 0.8 %multiply_reduce_fusion = s32[28]{0:T(128)S(1)} fusion(s32[28,28]{1,0:T(8,128)} %constant.104.clone, s32[28]{0:T(128)S(1)} %and_select_fusion.2), kind=kLoop, calls=%fused_computation.13 | loop fusion | flops 1540 | bytes 3360 | tf_op jit(solution)/shard_map/reduce_sum | solution.py:59
  7.2 0.1 fusion.4
  7.3 0.7 add_convert_fusion.ftab
  8.0 0.1 fusion.3
  8.1 1.1 %convert_reduce_fusion = s32[264]{0:T(512)S(1)} fusion(pred[264,264]{1,0:T(8,128)(4,1)} %constant.106.clone, s32[264]{0:T(512)S(1)} %pad_add_fusion), kind=kLoop, calls=%fused_computation.1 | loop fusion | flops 278520 | bytes 71808 | tf_op jit(solution)/shard_map/reduce_sum | solution.py:62
  9.2 0.8 %select_reduce_fusion = s32[292]{0:T(512)S(1)} fusion(s32[264]{0:T(512)} %constant.107.clone, s32[264]{0:T(512)S(1)} %add.82), kind=kLoop, calls=%fused_computation | loop fusion | flops 230972 | bytes 3280 | tf_op jit(solution)/shard_map/reduce_sum | solution.py:65
  10.1 0.7 %add.91 = s32[28,12]{1,0:T(8,128)S(1)} broadcast(s32[28]{0:T(128)} %constant.112.clone), dimensions={0} | broadcast | bytes 1456 | tf_op jit(solution)/shard_map/add | solution.py:85
  10.8 0.1 add.92
  10.9 0.8 %copy.25 = s32[1,1,28,12]{3,2,1,0:T(8,128)S(1)} copy(s32[1,1,28,12]{2,1,3,0:T(1,128)} %param.17) | data formatting | bytes 2688 | tf_op args[2]
  11.7 0.1 squeeze.9
  11.8 0.7 %concatenate.10.tab = s32[1164]{0:T(1024)} concatenate(s32[292]{0:T(512)S(1)} %get-tuple-element.8, s32[292]{0:T(512)S(1)} %get-tuple-element.7, s32[96]{0:T(128)S(1)} %get-tuple-element.12, s32[96]{0:T(128)S(1)} %get-tuple-element.11, s32[28]{0:T(128)S(1)} %get-tuple-element.9, s32[24]{0:T(128)S(1)} %get-tuple-element.5, s32[336]{0:T(512)S(1)} %compare_select_fusion), dimensions={0} | concatenate | bytes 9312 | tf_op jit(solution)/shard_map/concatenate | solution.py:86
  12.5 52.7 %filter_step.1 = f32[32,3584]{1,0:T(8,128)} custom-call(s32[1164]{0:T(1024)} %concatenate.10.tab, f32[218]{0:T(256)} %add_convert_fusion.ftab, bf16[32,3584]{1,0:T(8,128)(2,1)} %bitcast.9, bf16[336,128,128]{2,1,0:T(8,128)(2,1)} %bitcast.7), custom_call_target="tpu_custom_call" | custom-call | tf_op jit(solution)/shard_map/filter_step/pallas_call | solution.py:321
  65.2 1.8 %copy.30 = f32[1,1,32,3584]{3,2,1,0:T(8,128)} copy(f32[1,1,32,3584]{3,2,1,0:T(8,128)} %bitcast.8) | data formatting | bytes 917504
  (12 shorter events, 0.1 us)
where the time goes:
time: 67.6 us; the launch traced here: 67 us
  Pallas kernels  52.7 us (78%)
  other arithmetic  8.01 us (12%)
  local copies, waits for them, and re-layouts  6.21 us (9%)
    pallas_call x1, Pallas kernels, body(): pl.pallas_call(kernel, out_shape=jax.ShapeDtypeStruct((NVEC, BLK * BS), f...  52.7 us
    unnamed x3, local copies, waits for them, and re-layouts  3.3 us
    reduce_sum x2, other arithmetic, sorted_lists(): rank = ((target[:, None] == target[None, :]) & earlier).astype(i32).sum(1)  2.02 us
    reduce_sum x2, other arithmetic, sorted_lists(): start = jnp.asarray(base, i32) + (pairs[:, None] * before).sum(0)  1.61 us
    reduce_sum x2, other arithmetic, sorted_lists(): jnp.where(place[:, None] == pos[None, :], jnp.asarray(order + 1, i32)[Non...  1.59 us

commit v1 on v0

v1 whole, which is shorter than its diff:
```python
import math

import jax
import jax.numpy as jnp
import numpy as np
from jax import lax
from jax.experimental import pallas as pl
from jax.experimental.pallas import tpu as pltpu
from jax.sharding import PartitionSpec as P

f32 = jnp.float32
bf16 = jnp.bfloat16
i32 = jnp.int32
MESH = pl.DeviceIdType.MESH

NVEC = 32
BS = 128
K = 12
K_IN = 9
RIM = 6
BLK = 28
RIM_ROWS = 4 * RIM
LOWER = 0.3
CENTER = (2.0 + LOWER) / 2.0
HALF = (2.0 - LOWER) / 2.0
OPP = (1, 0, 3, 2)

N_OWN = RIM_ROWS * K_IN + (BLK - RIM_ROWS) * K
N_RIM = RIM_ROWS * (K - K_IN)
OWN_PAIRS = (N_OWN + BLK) // 2
RIM_PAIRS = (N_RIM // 4 + RIM) // 2
T_GROUPS = 2
Z_CHIPS = 8
Y_CHIPS = 4

N_POS = 512
OWN_POS = 2 * OWN_PAIRS
CHUNK = 4
SEND_AT = 4
SEGS = BLK + RIM_ROWS


def own_index(b):
    return b * K_IN if b < RIM_ROWS else RIM_ROWS * K_IN + (b - RIM_ROWS) * K


def build_tables(pat_ref, tab_i, tab_f, tab_p, hot_t, padded):
    tab_i[...] = jnp.zeros_like(tab_i)
    tab_f[...] = jnp.zeros_like(tab_f)
    padded[...] = jnp.full((NVEC, BS), 200.0, f32)
    padded[0:BLK, 0:K] = pat_ref[...].astype(f32)
    lane = lax.broadcasted_iota(i32, (NVEC, BS), 1)
    row = lax.broadcasted_iota(i32, (NVEC, BS), 0)
    face = jnp.where(row >= RIM, 1.0, 0.0) + jnp.where(row >= 2 * RIM, 1.0, 0.0) + jnp.where(row >= 3 * RIM, 1.0, 0.0)
    t = padded[...]
    t = jnp.where((t >= BLK) & (t < 100), t + RIM * face, t)
    tab_p[...] = jnp.clip(jnp.where(t < BLK, t, t - BLK), 0.0, BLK - 1.0).astype(i32)
    rows = K * NVEC
    column = jnp.concatenate([jnp.broadcast_to(t[:, s : s + 1], (NVEC, BS)) for s in range(K)], axis=0)
    seg = lax.broadcasted_iota(i32, (rows, BS), 1).astype(f32)
    hot = jnp.where(column == seg, 1.0, 0.0)
    hot_t[...] = hot.T[0 : hot_t.shape[0]].astype(bf16)
    hot_b = hot.astype(bf16)
    lower = lax.broadcasted_iota(i32, (rows, rows), 0) > lax.broadcasted_iota(i32, (rows, rows), 1)
    before = jnp.dot(jnp.where(lower, 1.0, 0.0).astype(bf16), hot_b, preferred_element_type=f32)
    ones8 = jnp.ones((8, rows), bf16)
    count = jnp.dot(ones8, hot_b, preferred_element_type=f32)
    pairs = jnp.floor((count + 1.0) * 0.5)

    def group(e):
        total = jnp.zeros(e.shape, f32)
        for r in range(4):
            total = total + jnp.where(e >= BLK + r * RIM, 1.0, 0.0)
        return total

    e0 = lax.broadcasted_iota(i32, (BS, BS), 0)
    e1 = lax.broadcasted_iota(i32, (BS, BS), 1)
    earlier = jnp.where((e0 < e1) & (group(e0) == group(e1)), 1.0, 0.0).astype(bf16)
    e8 = lax.broadcasted_iota(i32, (8, BS), 1)
    g8 = group(e8)
    base = jnp.where(g8 > 0, OWN_PAIRS + (g8 - 1.0) * RIM_PAIRS, 0.0)
    start = jnp.dot(pairs.astype(bf16), earlier, preferred_element_type=f32) + base
    rank = jnp.sum(hot * before, axis=1, keepdims=True)
    first = jnp.sum(hot * (2.0 * start[0:1]), axis=1, keepdims=True)
    valid = column[:, 0:1] < 100.0
    pos = jnp.where(valid, rank + first, -1.0)
    place = lax.broadcasted_iota(i32, (rows, N_POS), 1).astype(f32)
    at = jnp.where(pos == place, 1.0, 0.0)
    entry = lax.broadcasted_iota(i32, (8, rows), 1)
    which = lax.broadcasted_iota(i32, (8, rows), 0)
    vals = jnp.where(which == 0, (entry & 31) + 1, jnp.where(which == 1, entry >> 5, 0)).astype(f32).astype(bf16)
    found = jnp.dot(vals, at.astype(bf16), preferred_element_type=f32)
    opens = jnp.dot(ones8, jnp.where(rank == 0.0, at, 0.0).astype(bf16), preferred_element_type=f32)
    b = found[0:1] - 1.0
    s = found[1:2]
    p = lax.broadcasted_iota(i32, (1, N_POS), 1)
    own_w = jnp.where(b < RIM_ROWS, b * K_IN + s, RIM_ROWS * K_IN + (b - RIM_ROWS) * K + s)
    rim_w = jnp.clip(b * (K - K_IN) + s - K_IN, 0.0, N_RIM - 1.0)
    w = jnp.where(p < OWN_POS, jnp.clip(own_w, 0.0, N_OWN - 1.0), rim_w)
    source = jnp.where(b >= 0, jnp.minimum(b, BLK - 1.0), float(BLK))
    end = start + pairs - 1.0
    end = jnp.where(g8 > 0, jnp.clip(end - OWN_PAIRS, 0.0, 4 * RIM_PAIRS - 1.0), jnp.clip(end, 0.0, OWN_PAIRS - 1.0))
    tab_i[0:1, :] = w.astype(i32)
    tab_i[1:2, :] = source.astype(i32)
    tab_i[2:3, 0:BS] = end[0:1].astype(i32)
    tab_f[0:1, :] = 1.0 - opens[0:1]
    tab_f[1:2, 0:BS] = jnp.where(count[0:1] > 0, 1.0, 0.0)


def kernel(
    tab, ftab, ptab, hot_t, start_ref, w_hbm, out_ref,
    wo, wr, wto, wtr, u, rim, recv_v, recv_t, send_t, recv_d, send_d,
    cur, prev, acc, inv, run_o, run_r, pack, ar1, ar2, ar3,
    sums, rowsum,
    w_sem, vs, vr, ts, tr, ds, dr, s1, r1, s2, r2, s3, r3,
):
    ni = lax.axis_index("narrow")
    wi = lax.axis_index("wide")
    n_narrow = lax.axis_size("narrow")
    n_wide = lax.axis_size("wide")
    north = lax.rem(ni + n_narrow - 1, n_narrow)
    south = lax.rem(ni + 1, n_narrow)
    west = lax.rem(wi + n_wide - 1, n_wide)
    east = lax.rem(wi + 1, n_wide)
    neighbours = ({"narrow": north}, {"narrow": south}, {"wide": west}, {"wide": east})
    has = (ni > 0, ni < n_narrow - 1, wi > 0, wi < n_wide - 1)
    wy = wi // Z_CHIPS
    wz = lax.rem(wi, Z_CHIPS)
    group1 = [{"narrow": lax.rem(ni + k, n_narrow)} for k in range(1, 8)]
    group2 = [{"wide": lax.rem(wi + k * Z_CHIPS, n_wide)} for k in range(1, Y_CHIPS)]
    group3 = [{"wide": wy * Z_CHIPS + lax.rem(wz + k, Z_CHIPS)} for k in range(1, Z_CHIPS)]

    barrier = pltpu.get_barrier_semaphore()
    greeted = [{"wide": west}, {"wide": east}] + group1 + group2 + group3
    for peer in greeted:
        pl.semaphore_signal(barrier, inc=1, device_id=peer, device_id_type=MESH)

    rim_copies = []
    for b in range(RIM_ROWS):
        n = K - K_IN
        rim_copies.append(pltpu.make_async_copy(
            w_hbm.at[pl.ds(b * K + K_IN, n)], wr.at[pl.ds(b * n, n)], w_sem.at[b]))
    own_copies = []
    for b in range(BLK):
        n = K_IN if b < RIM_ROWS else K
        own_copies.append(pltpu.make_async_copy(
            w_hbm.at[pl.ds(b * K, n)], wo.at[pl.ds(own_index(b), n)], w_sem.at[RIM_ROWS + b]))
    for copy in rim_copies + own_copies:
        copy.start()

    for a in range(3):
        u[a, BLK] = jnp.zeros((NVEC, BS), bf16)
    sums[...] = jnp.zeros_like(sums)

    def pair_product(lhs, w, at):
        left = jnp.concatenate([lhs(tab[1, at]), lhs(tab[1, at + 1])], axis=1)
        right = jnp.concatenate([w[tab[0, at]], w[tab[0, at + 1]]], axis=0)
        return jnp.dot(left, right, preferred_element_type=f32)

    def rim_out(lhs, d, put):
        run = None
        for q in range(d * RIM_PAIRS, (d + 1) * RIM_PAIRS):
            at = OWN_POS + 2 * q
            part = pair_product(lhs, wr, at)
            run = part if run is None else run * ftab[0, at] + part
            run_r[q] = run
        for j in range(RIM):
            e = BLK + d * RIM + j
            put(d, j, (run_r[tab[2, e]] * ftab[1, e]).astype(bf16))

    def own_back(lhs):
        per = OWN_PAIRS // T_GROUPS

        def body(g, run):
            for q in range(per):
                at = g * per + q
                part = pair_product(lhs, wo, 2 * at)
                run = run * ftab[0, 2 * at] + part
                run_o[at] = run
            return run

        lax.fori_loop(0, T_GROUPS, body, jnp.zeros((NVEC, BS), f32))

    ones8 = jnp.ones((8, K * BS), bf16)

    def column_sums(w, first, n, b, s0):
        wide = jnp.concatenate([w[first + s] for s in range(n)], axis=1)
        total = jnp.dot(ones8[:, :BS], wide, preferred_element_type=f32)
        for s in range(n):
            at = (s0 + s) * NVEC + b
            sums[at : at + 1] = total[0:1, s * BS : (s + 1) * BS]

    def row_sums(wt, first, n):
        return jnp.dot(ones8[:, : n * BS], wt[first : first + n].reshape(n * BS, BS), preferred_element_type=f32)

    def grouped_sums():
        high = sums[...].astype(bf16)
        low = (sums[...] - high.astype(f32)).astype(bf16)
        return jnp.dot(hot_t[...], high, preferred_element_type=f32) + jnp.dot(
            hot_t[...], low, preferred_element_type=f32)

    for copy in rim_copies:
        copy.wait()
    m = K - K_IN
    for b in range(RIM_ROWS):
        for s in range(m):
            wtr[b * m + s] = wr[b * m + s].T
        column_sums(wr, b * m, m, b, K_IN)
    degree_copies = []

    def send_degree():
        out = grouped_sums()
        for d in range(4):
            at = BLK + d * RIM
            send_d[d, 0:RIM] = out[at : at + RIM].astype(bf16)
        pl.semaphore_wait(barrier, len(greeted))
        for d in (2, 3, 0, 1):
            copy = pltpu.make_async_remote_copy(
                send_d.at[d], recv_d.at[OPP[d]], ds.at[d], dr.at[OPP[d]],
                device_id=neighbours[d], device_id_type=MESH)
            copy.start()
            degree_copies.append(copy)

    def own_row_sums(b):
        total = row_sums(wto, own_index(b), K_IN if b < RIM_ROWS else K)
        if b < RIM_ROWS:
            total = total + jnp.where(has[b // RIM], row_sums(wtr, b * m, m), 0.0)
        rowsum[b : b + 1] = total[0:1]

    rowsum[...] = jnp.ones_like(rowsum)
    send_d[...] = jnp.zeros_like(send_d)
    chunks = [range(c, c + CHUNK) for c in range(0, BLK, CHUNK)]
    for c, chunk in enumerate(chunks):
        for b in chunk:
            own_copies[b].wait()
        if c == SEND_AT:
            send_degree()
        for b in chunk:
            n = K_IN if b < RIM_ROWS else K
            for s in range(n):
                wto[own_index(b) + s] = wo[own_index(b) + s].T
            column_sums(wo, own_index(b), n, b, 0)
        if c > 0:
            for b in chunks[c - 1]:
                own_row_sums(b)
    for b in chunks[-1]:
        own_row_sums(b)
    back = grouped_sums()
    degree = rowsum[...] + back[0:NVEC]
    rowsum[...] = degree
    for copy in degree_copies:
        copy.wait_recv()
    for d in range(4):
        at = d * RIM
        arrived = jnp.where(has[d], recv_d[d].astype(f32), 0.0)
        rowsum[at : at + RIM] = rowsum[at : at + RIM] + arrived[0:RIM]
    inv[...] = 1.0 / jnp.sqrt(0.5 * rowsum[...])
    for b in range(BLK):
        x = start_ref[:, b * BS : (b + 1) * BS].astype(f32)
        cur[b] = x
        prev[b] = x
        u[0, b] = (inv[b : b + 1] * x).astype(bf16)
    for copy in degree_copies:
        copy.wait_send()
    def step(a, carry):
        copies = []
        for d in (2, 3, 0, 1):
            copy = pltpu.make_async_remote_copy(
                u.at[a, pl.ds(d * RIM, RIM)], recv_v.at[a, OPP[d]], vs.at[a, d], vr.at[a, OPP[d]],
                device_id=neighbours[d], device_id_type=MESH)
            copy.start()
            copies.append(copy)

        def put_terms(d, j, value):
            send_t[a, d, j] = value

        term_copies = []
        for pair in ((2, 3), (0, 1)):
            for d in pair:
                rim_out(lambda k: u[a, k], d, put_terms)
            for d in pair:
                copy = pltpu.make_async_remote_copy(
                    send_t.at[a, d], recv_t.at[a, OPP[d]], ts.at[a, d], tr.at[a, OPP[d]],
                    device_id=neighbours[d], device_id_type=MESH)
                copy.start()
                term_copies.append(copy)
        own_back(lambda k: u[a, k])
        for b in range(BLK):
            n = K_IN if b < RIM_ROWS else K
            o = own_index(b)
            left = jnp.concatenate([u[a, ptab[b, s]] for s in range(n)], axis=1)
            ahead = jnp.dot(left, wto[o : o + n].reshape(n * BS, BS), preferred_element_type=f32)
            acc[b] = ahead + run_o[tab[2, b]]
        for copy in copies:
            copy.wait_recv()
        for d in range(4):
            for j in range(RIM):
                rim[d * RIM + j] = jnp.where(has[d], recv_v[a, d, j], jnp.zeros((NVEC, BS), bf16))
        for b in range(RIM_ROWS):
            left = jnp.concatenate([rim[jnp.minimum(ptab[b, K_IN + s], RIM_ROWS - 1)] for s in range(m)], axis=1)
            acc[b] += jnp.dot(left, wtr[b * m : b * m + m].reshape(m * BS, BS), preferred_element_type=f32)
        for copy in term_copies:
            copy.wait_recv()
        alpha = jnp.where(a == 0, 1.0, 2.0).astype(f32) / HALF
        beta = jnp.where(a == 0, 0.0, 1.0).astype(f32)
        nxt = lax.rem(a + 1, 3)
        for b in range(BLK):
            total = acc[b]
            if b < RIM_ROWS:
                total = total + jnp.where(has[b // RIM], recv_t[a, b // RIM, b % RIM].astype(f32), 0.0)
            root = inv[b : b + 1]
            y = cur[b]
            new = alpha * ((y - (0.5 * root) * total) - CENTER * y) - beta * prev[b]
            prev[b] = y
            cur[b] = new
            acc[b] = root * new
        for copy in copies + term_copies:
            copy.wait_send()
        for b in range(BLK):
            u[nxt, b] = acc[b].astype(bf16)
        return carry

    lax.fori_loop(0, 3, step, 0)

    highs = [cur[b].astype(bf16) for b in range(BLK)]
    lows = [(cur[b] - highs[b].astype(f32)).astype(bf16) for b in range(BLK)]
    stacked = jnp.concatenate([jnp.concatenate(highs, axis=1), jnp.concatenate(lows, axis=1)], axis=0)
    product = lax.dot_general(stacked, stacked, (((1,), (1,)), ((), ())), preferred_element_type=f32)
    gram = product[:NVEC, :NVEC] + product[NVEC:, NVEC:] + product[:NVEC, NVEC:] + product[NVEC:, :NVEC]
    packed = jnp.concatenate([gram[8 * g : 8 * g + 8] for g in range(4)], axis=1)

    for group, landing, sends, recvs in ((group1, ar1, s1, r1), (group2, ar2, s2, r2), (group3, ar3, s3, r3)):
        slot = {id(ar1): 0, id(ar2): 1, id(ar3): 2}[id(landing)]
        pack[slot] = packed
        sent = []
        for k, peer in enumerate(group):
            copy = pltpu.make_async_remote_copy(
                pack.at[slot], landing.at[k], sends.at[k], recvs.at[k],
                device_id=peer, device_id_type=MESH)
            copy.start()
            sent.append(copy)
        for copy in sent:
            copy.wait_recv()
        for k in range(len(group)):
            packed = packed + landing[k]
        for copy in sent:
            copy.wait_send()

    lane = lax.broadcasted_iota(i32, (NVEC, BS), 1)
    row = lax.broadcasted_iota(i32, (NVEC, BS), 0)
    moved = jnp.concatenate([pltpu.roll(packed, (96 - 32 * g) % 128, 1) for g in range(4)], axis=0)
    m = jnp.where(lane >= 96, moved, jnp.where(lax.rem(lane, 32) == row, 1.0, 0.0))
    roots = jnp.zeros((NVEC, BS), f32)
    for k in range(NVEC):
        pivot = m[k : k + 1, :]
        d = jnp.broadcast_to(pivot[:, 96 + k : 97 + k], (1, BS))
        column = jnp.broadcast_to(m[:, 96 + k : 97 + k], (NVEC, BS))
        roots = jnp.where(row == k, lax.rsqrt(d), roots)
        m = m - jnp.where(row > k, column, 0.0) * (pivot * (1.0 / d))
    count = n_narrow * n_wide * BLK * BS
    solve = m * roots * math.sqrt(count)
    solve_high = solve.astype(bf16)
    solve_low = (solve - solve_high.astype(f32)).astype(bf16)
    left = jnp.where((lane >= 32) & (lane < 64), solve_low.astype(f32), solve_high.astype(f32))
    left = jnp.where(lane < 96, left, 0.0).astype(bf16)
    for b in range(BLK):
        right = jnp.concatenate([highs[b], highs[b], lows[b], lows[b]], axis=0)
        out_ref[:, b * BS : (b + 1) * BS] = jnp.dot(left, right, preferred_element_type=f32)


def tables(pattern):
    return pl.pallas_call(
        build_tables,
        out_shape=[
            jax.ShapeDtypeStruct((8, N_POS), i32),
            jax.ShapeDtypeStruct((8, N_POS), f32),
            jax.ShapeDtypeStruct((NVEC, BS), i32),
            jax.ShapeDtypeStruct((64, K * NVEC), bf16),
        ],
        in_specs=[pl.BlockSpec(memory_space=pltpu.VMEM)],
        out_specs=[pl.BlockSpec(memory_space=pltpu.VMEM)] * 4,
        scratch_shapes=[pltpu.VMEM((NVEC, BS), f32)],
        compiler_params=pltpu.CompilerParams(vmem_limit_bytes=16 * 2**20),
        name="index_tables",
    )(pattern)


def body(start_block, weights, pattern):
    dma = pltpu.SemaphoreType.DMA
    vmem = pltpu.VMEM
    out = pl.pallas_call(
        kernel,
        out_shape=jax.ShapeDtypeStruct((NVEC, BLK * BS), f32),
        in_specs=[
            pl.BlockSpec(memory_space=pltpu.SMEM),
            pl.BlockSpec(memory_space=pltpu.SMEM),
            pl.BlockSpec(memory_space=pltpu.SMEM),
            pl.BlockSpec(memory_space=pltpu.VMEM),
            pl.BlockSpec(memory_space=pltpu.VMEM),
            pl.BlockSpec(memory_space=pl.ANY),
        ],
        out_specs=pl.BlockSpec(memory_space=pltpu.VMEM),
        scratch_shapes=[
            vmem((N_OWN, BS, BS), bf16),
            vmem((N_RIM, BS, BS), bf16),
            vmem((N_OWN, BS, BS), bf16),
            vmem((N_RIM, BS, BS), bf16),
            vmem((3, BLK + 1, NVEC, BS), bf16),
            vmem((RIM_ROWS, NVEC, BS), bf16),
            vmem((3, 4, RIM, NVEC, BS), bf16),
            vmem((3, 4, RIM, NVEC, BS), bf16),
            vmem((3, 4, RIM, NVEC, BS), bf16),
            vmem((4, 8, BS), bf16),
            vmem((4, 8, BS), bf16),
            vmem((BLK, NVEC, BS), f32),
            vmem((BLK, NVEC, BS), f32),
            vmem((BLK, NVEC, BS), f32),
            vmem((NVEC, BS), f32),
            vmem((OWN_PAIRS, NVEC, BS), f32),
            vmem((4 * RIM_PAIRS, NVEC, BS), f32),
            vmem((3, 8, BS), f32),
            vmem((7, 8, BS), f32),
            vmem((3, 8, BS), f32),
            vmem((7, 8, BS), f32),
            vmem((K * NVEC, BS), f32),
            vmem((NVEC, BS), f32),
            dma((RIM_ROWS + BLK,)),
            dma((3, 4)),
            dma((3, 4)),
            dma((3, 4)),
            dma((3, 4)),
            dma((4,)),
            dma((4,)),
            dma((7,)),
            dma((7,)),
            dma((3,)),
            dma((3,)),
            dma((7,)),
            dma((7,)),
        ],
        compiler_params=pltpu.CompilerParams(
            collective_id=0, has_side_effects=True, vmem_limit_bytes=56 * 2**20
        ),
        name="filter_step",
    )(*tables(pattern[0, 0]), start_block[0, 0], weights.reshape(BLK * K, BS, BS))
    return out.reshape(1, 1, NVEC, BLK * BS)


def solution(mesh):
    placed = (
        P("narrow", "wide", None, None),
        P("narrow", "wide", None, None, None, None),
        P("narrow", "wide", None, None),
    )
    return jax.shard_map(
        body, mesh=mesh, in_specs=placed, out_specs=P("narrow", "wide", None, None), check_vma=False
    )
```

time: 67.6 us -> 55.5 us (0.82)
  other arithmetic: 8.01 us -> 0 us
  Pallas kernels: 52.7 us -> 50.3 us
  local copies, waits for them, and re-layouts: 6.21 us -> 5.03 us
    reduce_sum x10 -> x0, other arithmetic: 5.63 us -> none  [the longest x2 2.02 us: sorted_lists(): rank = ((target[:, None] == target[None, :]) & earlier).astype(i32).sum(1)]
    pallas_call x1, Pallas kernels: 52.7 us -> 49.5 us  [body(): pl.pallas_call(kernel, out_shape=jax.ShapeDtypeStruct((NVEC, BLK * BS), f...]
    unnamed x3 -> x10, local copies, waits for them, and re-layouts: 3.3 us -> 5.03 us
    add x4 -> x0, local copies, waits for them, and re-layouts: 1.01 us -> none  [the longest x2 0.83 us: tables(): source = jnp.where(pattern < BLK, pattern, pattern + facing)]
    slice x3 -> x0, local copies, waits for them, and re-layouts: 0.94 us -> none  [the longest x2 0.86 us: tables(): pattern[RIM_ROWS:].reshape(-1)]
    pallas_call x0 -> x1, Pallas kernels: none -> 0.79 us  [tables(): pl.pallas_call(build_tables, out_shape=[jax.ShapeDtypeStruct((8, N_POS),...]
    add x3 -> x0, other arithmetic: 0.7 us -> none  [the longest x1 0.69 us: tables(): pattern[:RIM_ROWS, K_IN:].reshape(-1) - BLK]
    max x2 -> x0, other arithmetic: 0.68 us -> none  [sorted_lists(): end = jnp.maximum(start + pairs - 1, 0)]
where the time goes in v1:
time: 55.5 us; the launch traced here: 55.3 us
  Pallas kernels  50.3 us (91%)
  local copies, waits for them, and re-layouts  5.03 us (9%)
    pallas_call x1, Pallas kernels, body(): pl.pallas_call(kernel, out_shape=jax.ShapeDtypeStruct((NVEC, BLK * BS), f...  49.5 us
    unnamed x10, local copies, waits for them, and re-layouts  5.03 us

profile of v1, /device:TPU:1, one launch (start us, length us, event | category | flops | bytes accessed | tf_op | source)
XLA Modules:
  0.0 55.3 jit_solution(14106077027093873519)
XLA Ops:
  0.0 0.8 %copy.4 = s32[1,1,28,12]{3,2,1,0:T(8,128)S(1)} copy(s32[1,1,28,12]{2,1,3,0:T(1,128)} %param.5) | data formatting | bytes 2688 | tf_op args[2]
  0.8 0.8 %index_tables.1 = (s32[8,512]{1,0:T(8,128)S(1)}, f32[8,512]{1,0:T(8,128)S(1)}, s32[32,128]{1,0:T(8,128)S(1)}, bf16[64,384]{1,0:T(8,128)(2,1)S(1)}) custom-call(s32[28,12]{1,0:T(8,128)S(1)} %bitcast.4), custom_call_target="tpu_custom_call" | custom-call | tf_op jit(solution)/shard_map/index_tables/pallas_call | solution.py:372
  1.6 0.0 copy-start
  1.6 0.6 %copy-done = bf16[64,384]{1,0:T(8,128)(2,1)} copy-done((bf16[64,384]{1,0:T(8,128)(2,1)}, bf16[64,384]{1,0:T(8,128)(2,1)S(1)}, u32[]{:S(2)}) %copy-start) | copy-done | bytes 49176
  2.2 0.0 copy-start.1
  2.2 0.6 %copy-done.1 = s32[8,512]{1,0:T(8,128)} copy-done((s32[8,512]{1,0:T(8,128)}, s32[8,512]{1,0:T(8,128)S(1)}, u32[]{:S(2)}) %copy-start.1) | copy-done | bytes 16408
  2.8 0.0 copy-start.2
  2.8 0.6 %copy-done.2 = f32[8,512]{1,0:T(8,128)} copy-done((f32[8,512]{1,0:T(8,128)}, f32[8,512]{1,0:T(8,128)S(1)}, u32[]{:S(2)}) %copy-start.2) | copy-done | bytes 16408
  3.4 0.0 copy-start.3
  3.4 0.6 %copy-done.3 = s32[32,128]{1,0:T(8,128)} copy-done((s32[32,128]{1,0:T(8,128)}, s32[32,128]{1,0:T(8,128)S(1)}, u32[]{:S(2)}) %copy-start.3) | copy-done | bytes 16408
  4.0 49.5 %filter_step.1 = f32[32,3584]{1,0:T(8,128)} custom-call(s32[8,512]{1,0:T(8,128)} %copy-done.1, f32[8,512]{1,0:T(8,128)} %copy-done.2, s32[32,128]{1,0:T(8,128)} %copy-done.3, bf16[64,384]{1,0:T(8,128)(2,1)} %copy-done, bf16[32,3584]{1,0:T(8,128)(2,1)} %bitcast.7, bf16[336,128,128]{2,1,0:T(8,128)(2,1)} %bitcast.5), custom_call_target="tpu_custom_call" | custom-call | tf_op jit(solution)/shard_map/filter_step/pallas_call | solution.py:391
  53.5 1.8 %copy.6 = f32[1,1,32,3584]{3,2,1,0:T(8,128)} copy(f32[1,1,32,3584]{3,2,1,0:T(8,128)} %bitcast.6) | data formatting | bytes 917504
Async XLA Ops:
  1.6 0.6 %copy-start = (bf16[64,384]{1,0:T(8,128)(2,1)}, bf16[64,384]{1,0:T(8,128)(2,1)S(1)}, u32[]{:S(2)}) copy-start(bf16[64,384]{1,0:T(8,128)(2,1)S(1)} %get-tuple-element.12.hot_t) | copy-start | bytes 147460
  2.2 0.6 %copy-start.1 = (s32[8,512]{1,0:T(8,128)}, s32[8,512]{1,0:T(8,128)S(1)}, u32[]{:S(2)}) copy-start(s32[8,512]{1,0:T(8,128)S(1)} %get-tuple-element.9.tab) | copy-start | bytes 49156
  2.8 0.6 %copy-start.2 = (f32[8,512]{1,0:T(8,128)}, f32[8,512]{1,0:T(8,128)S(1)}, u32[]{:S(2)}) copy-start(f32[8,512]{1,0:T(8,128)S(1)} %get-tuple-element.10.ftab) | copy-start | bytes 49156
  3.4 0.6 %copy-start.3 = (s32[32,128]{1,0:T(8,128)}, s32[32,128]{1,0:T(8,128)S(1)}, u32[]{:S(2)}) copy-start(s32[32,128]{1,0:T(8,128)S(1)} %get-tuple-element.11.ptab) | copy-start | bytes 49156

commit v2 on v1

--- a/solution.py
+++ b/solution.py
@@ -48,7 +48,11 @@
     tab_i[...] = jnp.zeros_like(tab_i)
     tab_f[...] = jnp.zeros_like(tab_f)
     padded[...] = jnp.full((NVEC, BS), 200.0, f32)
-    padded[0:BLK, 0:K] = pat_ref[...].astype(f32)
+    for k in range(K):
+        padded[k : k + 1, 0:BLK] = pat_ref[k].astype(f32)
+    turned = padded[...].T[0:NVEC]
+    padded[...] = jnp.full((NVEC, BS), 200.0, f32)
+    padded[:, 0:NVEC] = turned
     lane = lax.broadcasted_iota(i32, (NVEC, BS), 1)
     row = lax.broadcasted_iota(i32, (NVEC, BS), 0)
     face = jnp.where(row >= RIM, 1.0, 0.0) + jnp.where(row >= 2 * RIM, 1.0, 0.0) + jnp.where(row >= 3 * RIM, 1.0, 0.0)
@@ -108,11 +112,11 @@
 
 
 def kernel(
-    tab, ftab, ptab, hot_t, start_ref, w_hbm, out_ref,
+    tab, ftab, ptab, hot_t, start_ref, w_hbm, solve_ref, cur,
     wo, wr, wto, wtr, u, rim, recv_v, recv_t, send_t, recv_d, send_d,
-    cur, prev, acc, inv, run_o, run_r, pack, ar1, ar2, ar3,
-    sums, rowsum,
-    w_sem, vs, vr, ts, tr, ds, dr, s1, r1, s2, r2, s3, r3,
+    prev, acc, inv, run_o, run_r, pack, ar1, ar2, ar3,
+    sums, rowsum, recv_x, send_i, recv_i,
+    w_sem, xs, xr, rs, rr, vs, vr, ts, tr, ds, dr, s1, r1, s2, r2, s3, r3,
 ):
     ni = lax.axis_index("narrow")
     wi = lax.axis_index("wide")
@@ -207,6 +211,7 @@
             wtr[b * m + s] = wr[b * m + s].T
         column_sums(wr, b * m, m, b, K_IN)
     degree_copies = []
+    start_copies = []
 
     def send_degree():
         out = grouped_sums()
@@ -220,6 +225,12 @@
                 device_id=neighbours[d], device_id_type=MESH)
             copy.start()
             degree_copies.append(copy)
+        for d in (2, 3, 0, 1):
+            copy = pltpu.make_async_remote_copy(
+                start_ref.at[:, pl.ds(d * RIM * BS, RIM * BS)], recv_x.at[OPP[d]], xs.at[d], xr.at[OPP[d]],
+                device_id=neighbours[d], device_id_type=MESH)
+            copy.start()
+            start_copies.append(copy)
 
     def own_row_sums(b):
         total = row_sums(wto, own_index(b), K_IN if b < RIM_ROWS else K)
@@ -229,6 +240,7 @@
 
     rowsum[...] = jnp.ones_like(rowsum)
     send_d[...] = jnp.zeros_like(send_d)
+    send_i[...] = jnp.zeros_like(send_i)
     chunks = [range(c, c + CHUNK) for c in range(0, BLK, CHUNK)]
     for c, chunk in enumerate(chunks):
         for b in chunk:
@@ -255,6 +267,15 @@
         arrived = jnp.where(has[d], recv_d[d].astype(f32), 0.0)
         rowsum[at : at + RIM] = rowsum[at : at + RIM] + arrived[0:RIM]
     inv[...] = 1.0 / jnp.sqrt(0.5 * rowsum[...])
+    root_copies = []
+    for d in (2, 3, 0, 1):
+        send_i[d, 0:RIM] = inv[d * RIM : d * RIM + RIM]
+    for d in (2, 3, 0, 1):
+        copy = pltpu.make_async_remote_copy(
+            send_i.at[d], recv_i.at[OPP[d]], rs.at[d], rr.at[OPP[d]],
+            device_id=neighbours[d], device_id_type=MESH)
+        copy.start()
+        root_copies.append(copy)
     for b in range(BLK):
         x = start_ref[:, b * BS : (b + 1) * BS].astype(f32)
         cur[b] = x
@@ -265,11 +286,14 @@
     def step(a, carry):
         copies = []
         for d in (2, 3, 0, 1):
-            copy = pltpu.make_async_remote_copy(
+            copies.append(pltpu.make_async_remote_copy(
                 u.at[a, pl.ds(d * RIM, RIM)], recv_v.at[a, OPP[d]], vs.at[a, d], vr.at[a, OPP[d]],
-                device_id=neighbours[d], device_id_type=MESH)
-            copy.start()
-            copies.append(copy)
+                device_id=neighbours[d], device_id_type=MESH))
+
+        @pl.when(a > 0)
+        def _():
+            for copy in copies:
+                copy.start()
 
         def put_terms(d, j, value):
             send_t[a, d, j] = value
@@ -291,11 +315,24 @@
             left = jnp.concatenate([u[a, ptab[b, s]] for s in range(n)], axis=1)
             ahead = jnp.dot(left, wto[o : o + n].reshape(n * BS, BS), preferred_element_type=f32)
             acc[b] = ahead + run_o[tab[2, b]]
-        for copy in copies:
-            copy.wait_recv()
-        for d in range(4):
-            for j in range(RIM):
-                rim[d * RIM + j] = jnp.where(has[d], recv_v[a, d, j], jnp.zeros((NVEC, BS), bf16))
+        @pl.when(a == 0)
+        def _():
+            for copy in start_copies + root_copies:
+                copy.wait()
+            for d in range(4):
+                for j in range(RIM):
+                    x = recv_x[d, :, j * BS : (j + 1) * BS].astype(f32)
+                    x = jnp.where(has[d], recv_i[d, j : j + 1] * x, 0.0)
+                    rim[d * RIM + j] = x.astype(bf16)
+
+        @pl.when(a > 0)
+        def _():
+            for copy in copies:
+                copy.wait()
+            for d in range(4):
+                for j in range(RIM):
+                    rim[d * RIM + j] = jnp.where(has[d], recv_v[a, d, j], jnp.zeros((NVEC, BS), bf16))
+
         for b in range(RIM_ROWS):
             left = jnp.concatenate([rim[jnp.minimum(ptab[b, K_IN + s], RIM_ROWS - 1)] for s in range(m)], axis=1)
             acc[b] += jnp.dot(left, wtr[b * m : b * m + m].reshape(m * BS, BS), preferred_element_type=f32)
@@ -314,7 +351,7 @@
             prev[b] = y
             cur[b] = new
             acc[b] = root * new
-        for copy in copies + term_copies:
+        for copy in term_copies:
             copy.wait_send()
         for b in range(BLK):
             u[nxt, b] = acc[b].astype(bf16)
@@ -351,20 +388,39 @@
     moved = jnp.concatenate([pltpu.roll(packed, (96 - 32 * g) % 128, 1) for g in range(4)], axis=0)
     m = jnp.where(lane >= 96, moved, jnp.where(lax.rem(lane, 32) == row, 1.0, 0.0))
     roots = jnp.zeros((NVEC, BS), f32)
-    for k in range(NVEC):
-        pivot = m[k : k + 1, :]
-        d = jnp.broadcast_to(pivot[:, 96 + k : 97 + k], (1, BS))
-        column = jnp.broadcast_to(m[:, 96 + k : 97 + k], (NVEC, BS))
-        roots = jnp.where(row == k, lax.rsqrt(d), roots)
-        m = m - jnp.where(row > k, column, 0.0) * (pivot * (1.0 / d))
+    for k in range(0, NVEC, 2):
+        top = m[k : k + 1]
+        low = m[k + 1 : k + 2]
+
+        def spread(line, j):
+            return jnp.broadcast_to(line[:, 96 + j : 97 + j], line.shape)
+
+        d0 = spread(top, k)
+        ratio = spread(top, k + 1) * (1.0 / d0)
+        d1 = spread(low, k + 1) - spread(top, k + 1) * ratio
+        second = low - ratio * top
+        c0 = spread(m, k)
+        c1 = spread(m, k + 1) - c0 * ratio
+        roots = jnp.where(row == k, lax.rsqrt(d0), jnp.where(row == k + 1, lax.rsqrt(d1), roots))
+        lower = m - c0 * (top * (1.0 / d0)) - c1 * (second * (1.0 / d1))
+        m = jnp.where(row > k + 1, lower, jnp.where(row == k + 1, second, m))
     count = n_narrow * n_wide * BLK * BS
     solve = m * roots * math.sqrt(count)
+    solve_ref[...] = solve
+
+
+def last_kernel(solve_ref, y_ref, out_ref):
+    solve = solve_ref[...]
+    lane = lax.broadcasted_iota(i32, (NVEC, BS), 1)
     solve_high = solve.astype(bf16)
     solve_low = (solve - solve_high.astype(f32)).astype(bf16)
     left = jnp.where((lane >= 32) & (lane < 64), solve_low.astype(f32), solve_high.astype(f32))
     left = jnp.where(lane < 96, left, 0.0).astype(bf16)
-    for b in range(BLK):
-        right = jnp.concatenate([highs[b], highs[b], lows[b], lows[b]], axis=0)
+    for b in range(y_ref.shape[0]):
+        y = y_ref[b]
+        high = y.astype(bf16)
+        low = (y - high.astype(f32)).astype(bf16)
+        right = jnp.concatenate([high, high, low, low], axis=0)
         out_ref[:, b * BS : (b + 1) * BS] = jnp.dot(left, right, preferred_element_type=f32)
 
 
@@ -372,10 +428,10 @@
     return pl.pallas_call(
         build_tables,
         out_shape=[
-            jax.ShapeDtypeStruct((8, N_POS), i32),
-            jax.ShapeDtypeStruct((8, N_POS), f32),
-            jax.ShapeDtypeStruct((NVEC, BS), i32),
-            jax.ShapeDtypeStruct((64, K * NVEC), bf16),
+            pltpu.HBM((8, N_POS), i32),
+            pltpu.HBM((8, N_POS), f32),
+            pltpu.HBM((NVEC, BS), i32),
+            pltpu.HBM((64, K * NVEC), bf16),
         ],
         in_specs=[pl.BlockSpec(memory_space=pltpu.VMEM)],
         out_specs=[pl.BlockSpec(memory_space=pltpu.VMEM)] * 4,
@@ -388,9 +444,12 @@
 def body(start_block, weights, pattern):
     dma = pltpu.SemaphoreType.DMA
     vmem = pltpu.VMEM
-    out = pl.pallas_call(
+    solve, final = pl.pallas_call(
         kernel,
-        out_shape=jax.ShapeDtypeStruct((NVEC, BLK * BS), f32),
+        out_shape=[
+            vmem((NVEC, BS), f32),
+            vmem((BLK, NVEC, BS), f32),
+        ],
         in_specs=[
             pl.BlockSpec(memory_space=pltpu.SMEM),
             pl.BlockSpec(memory_space=pltpu.SMEM),
@@ -399,7 +458,7 @@
             pl.BlockSpec(memory_space=pltpu.VMEM),
             pl.BlockSpec(memory_space=pl.ANY),
         ],
-        out_specs=pl.BlockSpec(memory_space=pltpu.VMEM),
+        out_specs=[pl.BlockSpec(memory_space=pltpu.VMEM)] * 2,
         scratch_shapes=[
             vmem((N_OWN, BS, BS), bf16),
             vmem((N_RIM, BS, BS), bf16),
@@ -414,7 +473,6 @@
             vmem((4, 8, BS), bf16),
             vmem((BLK, NVEC, BS), f32),
             vmem((BLK, NVEC, BS), f32),
-            vmem((BLK, NVEC, BS), f32),
             vmem((NVEC, BS), f32),
             vmem((OWN_PAIRS, NVEC, BS), f32),
             vmem((4 * RIM_PAIRS, NVEC, BS), f32),
@@ -424,7 +482,14 @@
             vmem((7, 8, BS), f32),
             vmem((K * NVEC, BS), f32),
             vmem((NVEC, BS), f32),
+            vmem((4, NVEC, RIM * BS), bf16),
+            vmem((4, 8, BS), f32),
+            vmem((4, 8, BS), f32),
             dma((RIM_ROWS + BLK,)),
+            dma((4,)),
+            dma((4,)),
+            dma((4,)),
+            dma((4,)),
             dma((3, 4)),
             dma((3, 4)),
             dma((3, 4)),
@@ -442,7 +507,19 @@
             collective_id=0, has_side_effects=True, vmem_limit_bytes=56 * 2**20
         ),
         name="filter_step",
-    )(*tables(pattern[0, 0]), start_block[0, 0], weights.reshape(BLK * K, BS, BS))
+    )(*tables(jnp.transpose(pattern, (0, 3, 1, 2)).reshape(K, 1, BLK)), start_block[0, 0], weights.reshape(BLK * K, BS, BS))
+    out = pl.pallas_call(
+        last_kernel,
+        grid=(BLK // CHUNK,),
+        out_shape=jax.ShapeDtypeStruct((NVEC, BLK * BS), f32),
+        in_specs=[
+            pl.BlockSpec((NVEC, BS), lambda i: (0, 0)),
+            pl.BlockSpec((CHUNK, NVEC, BS), lambda i: (i, 0, 0)),
+        ],
+        out_specs=pl.BlockSpec((NVEC, CHUNK * BS), lambda i: (0, i)),
+        compiler_params=pltpu.CompilerParams(vmem_limit_bytes=8 * 2**20),
+        name="last_product",
+    )(solve, final)
     return out.reshape(1, 1, NVEC, BLK * BS)
 
 

time: 55.5 us -> 52.6 us (0.948)
  local copies, waits for them, and re-layouts: 5.03 us -> 0.69 us
  Pallas kernels: 50.3 us -> 51.7 us
    unnamed x10 -> x2, local copies, waits for them, and re-layouts: 5.03 us -> 0.69 us
    pallas_call x2 -> x3, Pallas kernels: 50.3 us -> 51.7 us  [the longest x1 47 us: body(): pl.pallas_call(kernel, out_shape=[vmem((NVEC, BS), f32), vmem((BLK, NVEC,...]
where the time goes in v2:
time: 52.6 us; the launch traced here: 52.4 us
  Pallas kernels  51.7 us (98%)
  local copies, waits for them, and re-layouts  0.69 us (1%)
    pallas_call x1, Pallas kernels, body(): pl.pallas_call(kernel, out_shape=[vmem((NVEC, BS), f32), vmem((BLK, NVEC,...  47 us
    pallas_call x1, Pallas kernels, body(): pl.pallas_call(last_kernel, grid=(BLK // CHUNK,), out_shape=jax.ShapeDtyp...  3.16 us
    pallas_call x1, Pallas kernels, tables(): pl.pallas_call(build_tables, out_shape=[pltpu.HBM((8, N_POS), i32), pltpu...  1.49 us

profile of v2, /device:TPU:1, one launch (start us, length us, event | category | flops | bytes accessed | tf_op | source)
XLA Modules:
  0.0 52.4 jit_solution(4505839865994204656)
XLA Ops:
  0.0 0.0 copy-start
  0.0 0.7 %copy-done = s32[1,1,28,12]{2,1,3,0:T(1,128)S(1)} copy-done((s32[1,1,28,12]{2,1,3,0:T(1,128)S(1)}, s32[1,1,28,12]{2,1,3,0:T(1,128)}, u32[]{:S(2)}) %copy-start) | copy-done | bytes 1368
  0.7 1.5 %index_tables.1 = (s32[8,512]{1,0:T(8,128)}, f32[8,512]{1,0:T(8,128)}, s32[32,128]{1,0:T(8,128)}, bf16[64,384]{1,0:T(8,128)(2,1)}) custom-call(s32[12,1,28]{2,1,0:T(1,128)S(1)} %bitcast.6), custom_call_target="tpu_custom_call" | custom-call | tf_op jit(solution)/shard_map/index_tables/pallas_call | solution.py:428
  2.2 47.0 %filter_step.1 = (f32[32,128]{1,0:T(8,128)S(1)}, f32[28,32,128]{2,1,0:T(8,128)S(1)}) custom-call(s32[8,512]{1,0:T(8,128)} %get-tuple-element.11.tab, f32[8,512]{1,0:T(8,128)} %get-tuple-element.12.ftab, s32[32,128]{1,0:T(8,128)} %get-tuple-element.13.ptab, bf16[64,384]{1,0:T(8,128)(2,1)} %get-tuple-element.14.hot_t, bf16[32,3584]{1,0:T(8,128)(2,1)} %bitcast.8, ...), custom_call_target="tpu_custom_call" | custom-call | tf_op jit(solution)/shard_map/filter_step/pallas_call | solution.py:447
  49.2 3.2 %last_product.1 = f32[32,3584]{1,0:T(8,128)} custom-call(f32[32,128]{1,0:T(8,128)S(1)} %get-tuple-element.15.solve_ref, f32[28,32,128]{2,1,0:T(8,128)S(1)} %get-tuple-element.16.y_ref), custom_call_target="tpu_custom_call" | custom-call | tf_op jit(solution)/shard_map/last_product/pallas_call | solution.py:511
Async XLA Ops:
  0.0 0.7 %copy-start = (s32[1,1,28,12]{2,1,3,0:T(1,128)S(1)}, s32[1,1,28,12]{2,1,3,0:T(1,128)}, u32[]{:S(2)}) copy-start(s32[1,1,28,12]{2,1,3,0:T(1,128)} %param.5) | copy-start | bytes 4036

commit v3 on v2

--- a/solution.py
+++ b/solution.py
@@ -35,8 +35,9 @@
 
 N_POS = 512
 OWN_POS = 2 * OWN_PAIRS
-CHUNK = 4
-SEND_AT = 4
+CHUNK = 7
+SEND_AT = 2
+OUT_PARTS = 4
 SEGS = BLK + RIM_ROWS
 
 
@@ -112,11 +113,11 @@
 
 
 def kernel(
-    tab, ftab, ptab, hot_t, start_ref, w_hbm, solve_ref, cur,
+    tab_hbm, ftab_hbm, ptab_hbm, hot_hbm, start_hbm, w_hbm, solve_ref, cur,
     wo, wr, wto, wtr, u, rim, recv_v, recv_t, send_t, recv_d, send_d,
     prev, acc, inv, run_o, run_r, pack, ar1, ar2, ar3,
-    sums, rowsum, recv_x, send_i, recv_i,
-    w_sem, xs, xr, rs, rr, vs, vr, ts, tr, ds, dr, s1, r1, s2, r2, s3, r3,
+    sums, rowsum, recv_x, send_i, recv_i, tab, ftab, ptab, hot_t, start_ref,
+    w_sem, t_sem, xs, xr, rs, rr, vs, vr, ts, tr, ds, dr, s1, r1, s2, r2, s3, r3,
 ):
     ni = lax.axis_index("narrow")
     wi = lax.axis_index("wide")
@@ -130,9 +131,9 @@
     has = (ni > 0, ni < n_narrow - 1, wi > 0, wi < n_wide - 1)
     wy = wi // Z_CHIPS
     wz = lax.rem(wi, Z_CHIPS)
-    group1 = [{"narrow": lax.rem(ni + k, n_narrow)} for k in range(1, 8)]
-    group2 = [{"wide": lax.rem(wi + k * Z_CHIPS, n_wide)} for k in range(1, Y_CHIPS)]
-    group3 = [{"wide": wy * Z_CHIPS + lax.rem(wz + k, Z_CHIPS)} for k in range(1, Z_CHIPS)]
+    group1 = [{"narrow": lax.rem(ni + k, n_narrow)} for k in (4, 3, 5, 2, 6, 1, 7)]
+    group2 = [{"wide": lax.rem(wi + k * Z_CHIPS, n_wide)} for k in (2, 1, 3)]
+    group3 = [{"wide": wy * Z_CHIPS + lax.rem(wz + k, Z_CHIPS)} for k in (4, 3, 5, 2, 6, 1, 7)]
 
     barrier = pltpu.get_barrier_semaphore()
     greeted = [{"wide": west}, {"wide": east}] + group1 + group2 + group3
@@ -149,7 +150,12 @@
         n = K_IN if b < RIM_ROWS else K
         own_copies.append(pltpu.make_async_copy(
             w_hbm.at[pl.ds(b * K, n)], wo.at[pl.ds(own_index(b), n)], w_sem.at[RIM_ROWS + b]))
-    for copy in rim_copies + own_copies:
+    table_copies = [
+        pltpu.make_async_copy(source, target, t_sem.at[k])
+        for k, (source, target) in enumerate(
+            ((hot_hbm, hot_t), (start_hbm, start_ref), (tab_hbm, tab), (ftab_hbm, ftab), (ptab_hbm, ptab)))
+    ]
+    for copy in rim_copies + table_copies[:2] + own_copies + table_copies[2:]:
         copy.start()
 
     for a in range(3):
@@ -214,6 +220,8 @@
     start_copies = []
 
     def send_degree():
+        for copy in table_copies[:2]:
+            copy.wait()
         out = grouped_sums()
         for d in range(4):
             at = BLK + d * RIM
@@ -267,6 +275,8 @@
         arrived = jnp.where(has[d], recv_d[d].astype(f32), 0.0)
         rowsum[at : at + RIM] = rowsum[at : at + RIM] + arrived[0:RIM]
     inv[...] = 1.0 / jnp.sqrt(0.5 * rowsum[...])
+    for copy in table_copies[2:]:
+        copy.wait()
     root_copies = []
     for d in (2, 3, 0, 1):
         send_i[d, 0:RIM] = inv[d * RIM : d * RIM + RIM]
@@ -315,46 +325,57 @@
             left = jnp.concatenate([u[a, ptab[b, s]] for s in range(n)], axis=1)
             ahead = jnp.dot(left, wto[o : o + n].reshape(n * BS, BS), preferred_element_type=f32)
             acc[b] = ahead + run_o[tab[2, b]]
-        @pl.when(a == 0)
-        def _():
-            for copy in start_copies + root_copies:
-                copy.wait()
-            for d in range(4):
-                for j in range(RIM):
-                    x = recv_x[d, :, j * BS : (j + 1) * BS].astype(f32)
-                    x = jnp.where(has[d], recv_i[d, j : j + 1] * x, 0.0)
-                    rim[d * RIM + j] = x.astype(bf16)
-
-        @pl.when(a > 0)
-        def _():
-            for copy in copies:
-                copy.wait()
-            for d in range(4):
-                for j in range(RIM):
-                    rim[d * RIM + j] = jnp.where(has[d], recv_v[a, d, j], jnp.zeros((NVEC, BS), bf16))
-
-        for b in range(RIM_ROWS):
-            left = jnp.concatenate([rim[jnp.minimum(ptab[b, K_IN + s], RIM_ROWS - 1)] for s in range(m)], axis=1)
-            acc[b] += jnp.dot(left, wtr[b * m : b * m + m].reshape(m * BS, BS), preferred_element_type=f32)
-        for copy in term_copies:
-            copy.wait_recv()
         alpha = jnp.where(a == 0, 1.0, 2.0).astype(f32) / HALF
         beta = jnp.where(a == 0, 0.0, 1.0).astype(f32)
         nxt = lax.rem(a + 1, 3)
-        for b in range(BLK):
-            total = acc[b]
-            if b < RIM_ROWS:
-                total = total + jnp.where(has[b // RIM], recv_t[a, b // RIM, b % RIM].astype(f32), 0.0)
-            root = inv[b : b + 1]
-            y = cur[b]
-            new = alpha * ((y - (0.5 * root) * total) - CENTER * y) - beta * prev[b]
-            prev[b] = y
-            cur[b] = new
-            acc[b] = root * new
-        for copy in term_copies:
-            copy.wait_send()
-        for b in range(BLK):
-            u[nxt, b] = acc[b].astype(bf16)
+
+        def land(pair):
+            mine = slice(0, 2) if pair == (2, 3) else slice(2, 4)
+
+            @pl.when(a == 0)
+            def _():
+                for copy in start_copies[mine] + root_copies[mine]:
+                    copy.wait()
+                for d in pair:
+                    for j in range(RIM):
+                        x = recv_x[d, :, j * BS : (j + 1) * BS].astype(f32)
+                        x = jnp.where(has[d], recv_i[d, j : j + 1] * x, 0.0)
+                        rim[d * RIM + j] = x.astype(bf16)
+
+            @pl.when(a > 0)
+            def _():
+                for copy in copies[mine]:
+                    copy.wait()
+                for d in pair:
+                    for j in range(RIM):
+                        rim[d * RIM + j] = jnp.where(has[d], recv_v[a, d, j], jnp.zeros((NVEC, BS), bf16))
+
+            for d in pair:
+                for b in range(d * RIM, (d + 1) * RIM):
+                    left = jnp.concatenate(
+                        [rim[jnp.minimum(ptab[b, K_IN + s], RIM_ROWS - 1)] for s in range(m)], axis=1)
+                    acc[b] += jnp.dot(left, wtr[b * m : b * m + m].reshape(m * BS, BS), preferred_element_type=f32)
+
+        def advance(blocks):
+            for b in blocks:
+                total = acc[b]
+                if b < RIM_ROWS:
+                    total = total + jnp.where(has[b // RIM], recv_t[a, b // RIM, b % RIM].astype(f32), 0.0)
+                root = inv[b : b + 1]
+                y = cur[b]
+                new = alpha * ((y - (0.5 * root) * total) - CENTER * y) - beta * prev[b]
+                prev[b] = y
+                cur[b] = new
+                u[nxt, b] = (root * new).astype(bf16)
+
+        land((0, 1))
+        land((2, 3))
+        for copy in term_copies[2:]:
+            copy.wait()
+        advance(list(range(2 * RIM)) + list(range(RIM_ROWS, BLK)))
+        for copy in term_copies[:2]:
+            copy.wait()
+        advance(range(2 * RIM, RIM_ROWS))
         return carry
 
     lax.fori_loop(0, 3, step, 0)
@@ -409,19 +430,27 @@
     solve_ref[...] = solve
 
 
-def last_kernel(solve_ref, y_ref, out_ref):
+def last_kernel(solve_ref, y_ref, out_hbm, held, sem):
     solve = solve_ref[...]
     lane = lax.broadcasted_iota(i32, (NVEC, BS), 1)
     solve_high = solve.astype(bf16)
     solve_low = (solve - solve_high.astype(f32)).astype(bf16)
     left = jnp.where((lane >= 32) & (lane < 64), solve_low.astype(f32), solve_high.astype(f32))
     left = jnp.where(lane < 96, left, 0.0).astype(bf16)
-    for b in range(y_ref.shape[0]):
-        y = y_ref[b]
-        high = y.astype(bf16)
-        low = (y - high.astype(f32)).astype(bf16)
-        right = jnp.concatenate([high, high, low, low], axis=0)
-        out_ref[:, b * BS : (b + 1) * BS] = jnp.dot(left, right, preferred_element_type=f32)
+    copies = []
+    for c in range(OUT_PARTS):
+        per = BLK // OUT_PARTS
+        for b in range(c * per, (c + 1) * per):
+            y = y_ref[b]
+            high = y.astype(bf16)
+            low = (y - high.astype(f32)).astype(bf16)
+            right = jnp.concatenate([high, high, low, low], axis=0)
+            held[:, b * BS : (b + 1) * BS] = jnp.dot(left, right, preferred_element_type=f32)
+        part = pl.ds(c * per * BS, per * BS)
+        copies.append(pltpu.make_async_copy(held.at[:, part], out_hbm.at[:, part], sem.at[c]))
+        copies[-1].start()
+    for copy in copies:
+        copy.wait()
 
 
 def tables(pattern):
@@ -451,13 +480,9 @@
             vmem((BLK, NVEC, BS), f32),
         ],
         in_specs=[
-            pl.BlockSpec(memory_space=pltpu.SMEM),
-            pl.BlockSpec(memory_space=pltpu.SMEM),
-            pl.BlockSpec(memory_space=pltpu.SMEM),
-            pl.BlockSpec(memory_space=pltpu.VMEM),
-            pl.BlockSpec(memory_space=pltpu.VMEM),
             pl.BlockSpec(memory_space=pl.ANY),
-        ],
+        ]
+        * 6,
         out_specs=[pl.BlockSpec(memory_space=pltpu.VMEM)] * 2,
         scratch_shapes=[
             vmem((N_OWN, BS, BS), bf16),
@@ -485,7 +510,13 @@
             vmem((4, NVEC, RIM * BS), bf16),
             vmem((4, 8, BS), f32),
             vmem((4, 8, BS), f32),
+            pltpu.SMEM((8, N_POS), i32),
+            pltpu.SMEM((8, N_POS), f32),
+            pltpu.SMEM((NVEC, BS), i32),
+            vmem((64, K * NVEC), bf16),
+            vmem((NVEC, BLK * BS), bf16),
             dma((RIM_ROWS + BLK,)),
+            dma((5,)),
             dma((4,)),
             dma((4,)),
             dma((4,)),
@@ -510,13 +541,10 @@
     )(*tables(jnp.transpose(pattern, (0, 3, 1, 2)).reshape(K, 1, BLK)), start_block[0, 0], weights.reshape(BLK * K, BS, BS))
     out = pl.pallas_call(
         last_kernel,
-        grid=(BLK // CHUNK,),
         out_shape=jax.ShapeDtypeStruct((NVEC, BLK * BS), f32),
-        in_specs=[
-            pl.BlockSpec((NVEC, BS), lambda i: (0, 0)),
-            pl.BlockSpec((CHUNK, NVEC, BS), lambda i: (i, 0, 0)),
-        ],
-        out_specs=pl.BlockSpec((NVEC, CHUNK * BS), lambda i: (0, i)),
+        in_specs=[pl.BlockSpec(memory_space=pltpu.VMEM)] * 2,
+        out_specs=pl.BlockSpec(memory_space=pl.ANY),
+        scratch_shapes=[vmem((NVEC, BLK * BS), f32), dma((OUT_PARTS,))],
         compiler_params=pltpu.CompilerParams(vmem_limit_bytes=8 * 2**20),
         name="last_product",
     )(solve, final)

time: 52.6 us -> 47.7 us (0.907)
  Pallas kernels: 51.7 us -> 46.9 us
    pallas_call x1, Pallas kernels: 47 us -> 44.4 us  [body(): pl.pallas_call(kernel, out_shape=[vmem((NVEC, BS), f32), vmem((BLK, NVEC,...]
    pallas_call x1, Pallas kernels: 3.16 us -> 1.04 us  [body(): pl.pallas_call(last_kernel, out_shape=jax.ShapeDtypeStruct((NVEC, BLK * B...]
where the time goes in v3:
time: 47.7 us; the launch traced here: 47.6 us
  Pallas kernels  46.9 us (98%)
  local copies, waits for them, and re-layouts  0.69 us (1%)
    pallas_call x1, Pallas kernels, body(): pl.pallas_call(kernel, out_shape=[vmem((NVEC, BS), f32), vmem((BLK, NVEC,...  44.4 us
    pallas_call x1, Pallas kernels, tables(): pl.pallas_call(build_tables, out_shape=[pltpu.HBM((8, N_POS), i32), pltpu...  1.49 us
    pallas_call x1, Pallas kernels, body(): pl.pallas_call(last_kernel, out_shape=jax.ShapeDtypeStruct((NVEC, BLK * B...  1.04 us

profile of v3, /device:TPU:1, one launch (start us, length us, event | category | flops | bytes accessed | tf_op | source)
XLA Modules:
  0.0 47.6 jit_solution(10074942681245270090)
XLA Ops:
  0.0 0.0 copy-start
  0.0 0.7 %copy-done = s32[1,1,28,12]{2,1,3,0:T(1,128)S(1)} copy-done((s32[1,1,28,12]{2,1,3,0:T(1,128)S(1)}, s32[1,1,28,12]{2,1,3,0:T(1,128)}, u32[]{:S(2)}) %copy-start) | copy-done | bytes 1368
  0.7 1.5 %index_tables.1 = (s32[8,512]{1,0:T(8,128)}, f32[8,512]{1,0:T(8,128)}, s32[32,128]{1,0:T(8,128)}, bf16[64,384]{1,0:T(8,128)(2,1)}) custom-call(s32[12,1,28]{2,1,0:T(1,128)S(1)} %bitcast.6), custom_call_target="tpu_custom_call" | custom-call | tf_op jit(solution)/shard_map/index_tables/pallas_call | solution.py:457
  2.2 44.4 %filter_step.1 = (f32[32,128]{1,0:T(8,128)S(1)}, f32[28,32,128]{2,1,0:T(8,128)S(1)}) custom-call(s32[8,512]{1,0:T(8,128)} %get-tuple-element.11.tab_hbm, f32[8,512]{1,0:T(8,128)} %get-tuple-element.12.ftab_hbm, s32[32,128]{1,0:T(8,128)} %get-tuple-element.13.ptab_hbm, bf16[64,384]{1,0:T(8,128)(2,1)} %get-tuple-element.14.hot_hbm, bf16[32,3584]{1,0:T(8,128)(2,1)} %bitcast.8, ...), custom_call_target="tpu_custom_call" | custom-call | tf_op jit(solution)/shard_map/filter_step/pallas_call | solution.py:476
  46.6 1.0 %last_product.1 = f32[32,3584]{1,0:T(8,128)} custom-call(f32[32,128]{1,0:T(8,128)S(1)} %get-tuple-element.15.solve_ref, f32[28,32,128]{2,1,0:T(8,128)S(1)} %get-tuple-element.16.y_ref), custom_call_target="tpu_custom_call" | custom-call | tf_op jit(solution)/shard_map/last_product/pallas_call | solution.py:542
Async XLA Ops:
  0.0 0.7 %copy-start = (s32[1,1,28,12]{2,1,3,0:T(1,128)S(1)}, s32[1,1,28,12]{2,1,3,0:T(1,128)}, u32[]{:S(2)}) copy-start(s32[1,1,28,12]{2,1,3,0:T(1,128)} %param.5) | copy-start | bytes 4036

commit v4 on v3

--- a/solution.py
+++ b/solution.py
@@ -59,7 +59,7 @@
     face = jnp.where(row >= RIM, 1.0, 0.0) + jnp.where(row >= 2 * RIM, 1.0, 0.0) + jnp.where(row >= 3 * RIM, 1.0, 0.0)
     t = padded[...]
     t = jnp.where((t >= BLK) & (t < 100), t + RIM * face, t)
-    tab_p[...] = jnp.clip(jnp.where(t < BLK, t, t - BLK), 0.0, BLK - 1.0).astype(i32)
+    tab_p[...] = jnp.clip(jnp.where(t < BLK, t, t - BLK).astype(i32), 0, BLK - 1)
     rows = K * NVEC
     column = jnp.concatenate([jnp.broadcast_to(t[:, s : s + 1], (NVEC, BS)) for s in range(K)], axis=0)
     seg = lax.broadcasted_iota(i32, (rows, BS), 1).astype(f32)
@@ -105,18 +105,19 @@
     source = jnp.where(b >= 0, jnp.minimum(b, BLK - 1.0), float(BLK))
     end = start + pairs - 1.0
     end = jnp.where(g8 > 0, jnp.clip(end - OWN_PAIRS, 0.0, 4 * RIM_PAIRS - 1.0), jnp.clip(end, 0.0, OWN_PAIRS - 1.0))
-    tab_i[0:1, :] = w.astype(i32)
-    tab_i[1:2, :] = source.astype(i32)
-    tab_i[2:3, 0:BS] = end[0:1].astype(i32)
+    tab_i[0:1, :] = jnp.clip(w.astype(i32), 0, jnp.where(p < OWN_POS, N_OWN - 1, N_RIM - 1))
+    tab_i[1:2, :] = jnp.clip(source.astype(i32), 0, BLK)
+    limit = jnp.where(e8[0:1] >= BLK, 4 * RIM_PAIRS - 1, OWN_PAIRS - 1)
+    tab_i[2:3, 0:BS] = jnp.clip(end[0:1].astype(i32), 0, limit)
     tab_f[0:1, :] = 1.0 - opens[0:1]
     tab_f[1:2, 0:BS] = jnp.where(count[0:1] > 0, 1.0, 0.0)
 
 
 def kernel(
-    tab_hbm, ftab_hbm, ptab_hbm, hot_hbm, start_hbm, w_hbm, solve_ref, cur,
+    pat_ref, start_hbm, w_hbm, solve_ref, cur,
     wo, wr, wto, wtr, u, rim, recv_v, recv_t, send_t, recv_d, send_d,
     prev, acc, inv, run_o, run_r, pack, ar1, ar2, ar3,
-    sums, rowsum, recv_x, send_i, recv_i, tab, ftab, ptab, hot_t, start_ref,
+    sums, rowsum, recv_x, send_i, recv_i, tab, ftab, ptab, hot_t, start_ref, tab_i, tab_f, tab_p, padded,
     w_sem, t_sem, xs, xr, rs, rr, vs, vr, ts, tr, ds, dr, s1, r1, s2, r2, s3, r3,
 ):
     ni = lax.axis_index("narrow")
@@ -150,12 +151,15 @@
         n = K_IN if b < RIM_ROWS else K
         own_copies.append(pltpu.make_async_copy(
             w_hbm.at[pl.ds(b * K, n)], wo.at[pl.ds(own_index(b), n)], w_sem.at[RIM_ROWS + b]))
+    start_copy = pltpu.make_async_copy(start_hbm, start_ref, t_sem.at[3])
+    for copy in rim_copies + [start_copy] + own_copies:
+        copy.start()
+    build_tables(pat_ref, tab_i, tab_f, tab_p, hot_t, padded)
     table_copies = [
         pltpu.make_async_copy(source, target, t_sem.at[k])
-        for k, (source, target) in enumerate(
-            ((hot_hbm, hot_t), (start_hbm, start_ref), (tab_hbm, tab), (ftab_hbm, ftab), (ptab_hbm, ptab)))
+        for k, (source, target) in enumerate(((tab_i, tab), (tab_f, ftab), (tab_p, ptab)))
     ]
-    for copy in rim_copies + table_copies[:2] + own_copies + table_copies[2:]:
+    for copy in table_copies:
         copy.start()
 
     for a in range(3):
@@ -220,8 +224,7 @@
     start_copies = []
 
     def send_degree():
-        for copy in table_copies[:2]:
-            copy.wait()
+        start_copy.wait()
         out = grouped_sums()
         for d in range(4):
             at = BLK + d * RIM
@@ -275,7 +278,7 @@
         arrived = jnp.where(has[d], recv_d[d].astype(f32), 0.0)
         rowsum[at : at + RIM] = rowsum[at : at + RIM] + arrived[0:RIM]
     inv[...] = 1.0 / jnp.sqrt(0.5 * rowsum[...])
-    for copy in table_copies[2:]:
+    for copy in table_copies:
         copy.wait()
     root_copies = []
     for d in (2, 3, 0, 1):
@@ -453,23 +456,6 @@
         copy.wait()
 
 
-def tables(pattern):
-    return pl.pallas_call(
-        build_tables,
-        out_shape=[
-            pltpu.HBM((8, N_POS), i32),
-            pltpu.HBM((8, N_POS), f32),
-            pltpu.HBM((NVEC, BS), i32),
-            pltpu.HBM((64, K * NVEC), bf16),
-        ],
-        in_specs=[pl.BlockSpec(memory_space=pltpu.VMEM)],
-        out_specs=[pl.BlockSpec(memory_space=pltpu.VMEM)] * 4,
-        scratch_shapes=[pltpu.VMEM((NVEC, BS), f32)],
-        compiler_params=pltpu.CompilerParams(vmem_limit_bytes=16 * 2**20),
-        name="index_tables",
-    )(pattern)
-
-
 def body(start_block, weights, pattern):
     dma = pltpu.SemaphoreType.DMA
     vmem = pltpu.VMEM
@@ -480,9 +466,10 @@
             vmem((BLK, NVEC, BS), f32),
         ],
         in_specs=[
+            pl.BlockSpec(memory_space=pltpu.VMEM),
             pl.BlockSpec(memory_space=pl.ANY),
-        ]
-        * 6,
+            pl.BlockSpec(memory_space=pl.ANY),
+        ],
         out_specs=[pl.BlockSpec(memory_space=pltpu.VMEM)] * 2,
         scratch_shapes=[
             vmem((N_OWN, BS, BS), bf16),
@@ -515,8 +502,12 @@
             pltpu.SMEM((NVEC, BS), i32),
             vmem((64, K * NVEC), bf16),
             vmem((NVEC, BLK * BS), bf16),
+            vmem((8, N_POS), i32),
+            vmem((8, N_POS), f32),
+            vmem((NVEC, BS), i32),
+            vmem((NVEC, BS), f32),
             dma((RIM_ROWS + BLK,)),
-            dma((5,)),
+            dma((4,)),
             dma((4,)),
             dma((4,)),
             dma((4,)),
@@ -538,7 +529,7 @@
             collective_id=0, has_side_effects=True, vmem_limit_bytes=56 * 2**20
         ),
         name="filter_step",
-    )(*tables(jnp.transpose(pattern, (0, 3, 1, 2)).reshape(K, 1, BLK)), start_block[0, 0], weights.reshape(BLK * K, BS, BS))
+    )(jnp.transpose(pattern, (0, 3, 1, 2)).reshape(K, 1, BLK), start_block[0, 0], weights.reshape(BLK * K, BS, BS))
     out = pl.pallas_call(
         last_kernel,
         out_shape=jax.ShapeDtypeStruct((NVEC, BLK * BS), f32),

time: 47.7 us -> 46.3 us (0.971)
  Pallas kernels: 46.9 us -> 46.2 us
  local copies, waits for them, and re-layouts: 0.69 us -> 0 us
    pallas_call x1 -> x0, Pallas kernels: 1.49 us -> none  [tables(): pl.pallas_call(build_tables, out_shape=[pltpu.HBM((8, N_POS), i32), pltpu...]
    pallas_call x1, Pallas kernels: 44.4 us -> 45.1 us  [body(): pl.pallas_call(kernel, out_shape=[vmem((NVEC, BS), f32), vmem((BLK, NVEC,...]
    unnamed x2 -> x0, local copies, waits for them, and re-layouts: 0.69 us -> none
where the time goes in v4:
time: 46.3 us; the launch traced here: 46.2 us
  Pallas kernels  46.2 us (100%)
    pallas_call x1, Pallas kernels, body(): pl.pallas_call(kernel, out_shape=[vmem((NVEC, BS), f32), vmem((BLK, NVEC,...  45.1 us
    pallas_call x1, Pallas kernels, body(): pl.pallas_call(last_kernel, out_shape=jax.ShapeDtypeStruct((NVEC, BLK * B...  1.04 us

profile of v4, /device:TPU:1, one launch (start us, length us, event | category | flops | bytes accessed | tf_op | source)
XLA Modules:
  0.0 46.2 jit_solution(6803382686250132815)
XLA Ops:
  0.0 45.1 %filter_step.1 = (f32[32,128]{1,0:T(8,128)S(1)}, f32[28,32,128]{2,1,0:T(8,128)S(1)}) custom-call(s32[12,1,28]{2,1,0:T(1,128)} %bitcast.8, bf16[32,3584]{1,0:T(8,128)(2,1)} %bitcast.7, bf16[336,128,128]{2,1,0:T(8,128)(2,1)} %bitcast.6), custom_call_target="tpu_custom_call" | custom-call | tf_op jit(solution)/shard_map/filter_step/pallas_call | solution.py:462
  45.2 1.0 %last_product.1 = f32[32,3584]{1,0:T(8,128)} custom-call(f32[32,128]{1,0:T(8,128)S(1)} %get-tuple-element.7.solve_ref, f32[28,32,128]{2,1,0:T(8,128)S(1)} %get-tuple-element.8.y_ref), custom_call_target="tpu_custom_call" | custom-call | tf_op jit(solution)/shard_map/last_product/pallas_call | solution.py:533

commit v5 on v4

--- a/solution.py
+++ b/solution.py
@@ -29,7 +29,7 @@
 N_RIM = RIM_ROWS * (K - K_IN)
 OWN_PAIRS = (N_OWN + BLK) // 2
 RIM_PAIRS = (N_RIM // 4 + RIM) // 2
-T_GROUPS = 2
+T_GROUPS = 1
 Z_CHIPS = 8
 Y_CHIPS = 4
 
@@ -271,6 +271,10 @@
     back = grouped_sums()
     degree = rowsum[...] + back[0:NVEC]
     rowsum[...] = degree
+    for b in range(BLK):
+        x = start_ref[:, b * BS : (b + 1) * BS].astype(f32)
+        cur[b] = x
+        prev[b] = x
     for copy in degree_copies:
         copy.wait_recv()
     for d in range(4):
@@ -290,10 +294,7 @@
         copy.start()
         root_copies.append(copy)
     for b in range(BLK):
-        x = start_ref[:, b * BS : (b + 1) * BS].astype(f32)
-        cur[b] = x
-        prev[b] = x
-        u[0, b] = (inv[b : b + 1] * x).astype(bf16)
+        u[0, b] = (inv[b : b + 1] * cur[b]).astype(bf16)
     for copy in degree_copies:
         copy.wait_send()
     def step(a, carry):

time: 46.3 us -> 46.2 us (level)
  no operation moved by 1% of the time
where the time goes in v5:
time: 46.2 us; the launch traced here: 46.1 us
  Pallas kernels  46.1 us (100%)
    pallas_call x1, Pallas kernels, body(): pl.pallas_call(kernel, out_shape=[vmem((NVEC, BS), f32), vmem((BLK, NVEC,...  45.1 us
    pallas_call x1, Pallas kernels, body(): pl.pallas_call(last_kernel, out_shape=jax.ShapeDtypeStruct((NVEC, BLK * B...  1.04 us

profile of v5, /device:TPU:1, one launch (start us, length us, event | category | flops | bytes accessed | tf_op | source)
XLA Modules:
  0.0 46.1 jit_solution(246930861060947414)
XLA Ops:
  0.0 45.1 %filter_step.1 = (f32[32,128]{1,0:T(8,128)S(1)}, f32[28,32,128]{2,1,0:T(8,128)S(1)}) custom-call(s32[12,1,28]{2,1,0:T(1,128)} %bitcast.8, bf16[32,3584]{1,0:T(8,128)(2,1)} %bitcast.7, bf16[336,128,128]{2,1,0:T(8,128)(2,1)} %bitcast.6), custom_call_target="tpu_custom_call" | custom-call | tf_op jit(solution)/shard_map/filter_step/pallas_call | solution.py:463
  45.1 1.0 %last_product.1 = f32[32,3584]{1,0:T(8,128)} custom-call(f32[32,128]{1,0:T(8,128)S(1)} %get-tuple-element.7.solve_ref, f32[28,32,128]{2,1,0:T(8,128)S(1)} %get-tuple-element.8.y_ref), custom_call_target="tpu_custom_call" | custom-call | tf_op jit(solution)/shard_map/last_product/pallas_call | solution.py:534
